TPU v7x, 32 devices: a whole 2x2x4 slice. The times are simulated.
32 devices in a mesh: sec: 2 (over x), col: 2 (over y), elem: 8 (over z, core).
Axes of the slice: x: 2, y: 2, z: 4, core: 2. Of those that a mesh axis runs over, the one named last changes fastest.
Arguments:
- probes: float32 [64, 48, 256], P('col', 'elem'), may hold values from -6 to 6
- jacobian: float32 [2, 48, 7, 256, 256], P('sec', 'elem'), may hold values from -0.0625 to 0.0625
- neighbors: int32 [48, 7], P('elem'), may hold values from 0 to 47, as said below
- stations: int32 [512], P('elem'), may hold values from 0 to 47, as said below
- obs_weights: float32 [512, 256], P('elem'), may hold values from -0.75 to 0.75
Outputs:
- hess_probes: float32 [64, 48, 256], P('col', 'elem', 'sec')
- gram: float32 [64, 64], P('col')
Inputs may be any that keep to these rules, and one draw needn't show every extreme that they name: `neighbors`: row e lists the 7 elements e - 3 to e + 3, taken modulo 48, each once, in an order drawn for each row. Station i lies in one of the 6 elements from (i // 64) * 6 on; every element holds one or more stations.
All inputs are finite; a program needn't handle non-finite values.
Results may differ from a plain program's by a relative error of at most 0.0001.
Values sent between devices are 32-bit elements; how exact they have to be, the bound alone decides.
A program may use at most 64 MiB of HBM per device.

v0:
```python
import functools
import math

import jax
import jax.numpy as jnp
from jax import lax
from jax.experimental import pallas as pl
from jax.experimental.pallas import tpu as pltpu
from jax.sharding import PartitionSpec as P

STEPS = 2
MESH = pl.DeviceIdType.MESH
F32 = jnp.float32
BF16 = jnp.bfloat16
LANES = 128


def halves(value):
    high = value.astype(BF16)
    low = (value - high.astype(F32)).astype(BF16)
    return high, low


def product(a, b, transposed):
    dims = (((1,), (1 if transposed else 0,)), ((), ()))
    return lax.dot_general(a, b, dims, preferred_element_type=F32)


def product3(stack, high, low, transposed):
    rows = stack.shape[0] // 2
    first = product(stack, high, transposed)
    second = product(stack[:rows], low, transposed)
    return first[:rows] + (first[rows:] + second)


def kernel(
    sizes,
    neighbors,
    stations,
    probes_hbm,
    jacobian_hbm,
    weights_hbm,
    hess_ref,
    gram_ref,
    *scratch,
):
    cols, elems, order, nbrs, stats, n_elem, n_col = sizes
    radius = (nbrs - 1) // 2
    width = radius * order
    half = order // 2
    jac_f32 = scratch[:elems]
    jac_high = scratch[elems : 2 * elems]
    jac_low = scratch[2 * elems : 3 * elems]
    (
        probes_ref, weights_ref, state, field, halo_left, halo_right,
        adjoint, adjoint_in, observed, out_left, out_right, back_left, back_right,
        back_across, out_half, back_half, readings, partial, partial_in, upper, upper_in,
        load_sem, send_sem, recv_sem,
    ) = scratch[3 * elems :]
    section = lax.axis_index("sec")
    column = lax.axis_index("col")
    block = lax.axis_index("elem")
    left = lax.rem(block + n_elem - 1, n_elem)
    right = lax.rem(block + 1, n_elem)
    even = lax.rem(block, 2) == 0
    far = jnp.where(even, left, right)
    other = 1 - section
    first_elem = block * elems
    elem_total = elems * n_elem
    rounds = int(math.log2(n_elem))
    edge = radius + elems
    full = elems * order
    last = STEPS - 1
    LEFT, RIGHT = 0, 1
    neighbour = (left, right)
    halo_in = (halo_left, halo_right)
    out = (out_left, out_right)
    back = (back_left, back_right)
    own = (slice(0, width), slice(full - width, full))
    own_ds = (pl.ds(0, width), pl.ds(full - width, width))
    own_elems = (range(0, radius), range(elems - radius, elems))
    own_span = ((radius, 2 * radius), (edge - radius, edge))

    def by_parity(run):
        @pl.when(even)
        def _():
            run(RIGHT, LEFT)

        @pl.when(jnp.logical_not(even))
        def _():
            run(LEFT, RIGHT)

    probe_load = pltpu.make_async_copy(probes_hbm, probes_ref, load_sem.at[elems])
    probe_load.start()
    jac_loads = [
        pltpu.make_async_copy(jacobian_hbm.at[0, e], jac_f32[e], load_sem.at[e])
        for e in range(elems)
    ]
    for load in jac_loads:
        load.start()
    weights_load = pltpu.make_async_copy(
        weights_hbm, weights_ref.at[pl.ds(0, stats)], load_sem.at[elems + 1]
    )
    weights_load.start()

    barrier = pltpu.get_barrier_semaphore()
    partners = [{"elem": left}, {"elem": right}, {"sec": other}, {"sec": other, "elem": far}]
    partners += [{"col": lax.rem(column + j, n_col)} for j in range(1, n_col)]
    flips = []
    for r in range(rounds):
        bit = 1 << r
        upper_bit = lax.rem(block // bit, 2)
        flips.append({"elem": block + bit - 2 * bit * upper_bit})
    for partner in partners + flips:
        pl.semaphore_signal(barrier, inc=1, device_id=partner, device_id_type=MESH)

    probe_load.wait()

    @pl.when(section == 0)
    def _():
        for e in range(elems):
            state[0, :, e * order : (e + 1) * order] = probes_ref[e]

    pl.semaphore_wait(barrier, len(partners) + len(flips))

    def remote(src, dst, index, target, arrival=None):
        arrival = index if arrival is None else arrival
        return pltpu.make_async_remote_copy(
            src_ref=src, dst_ref=dst, send_sem=send_sem.at[index],
            recv_sem=recv_sem.at[arrival], device_id=target, device_id_type=MESH,
        )

    FORWARD = 4 * STEPS
    BACKWARD, UPPER = FORWARD + 2, FORWARD + 4
    ACROSS, RETURN, GRAM, LOWER, HIGHER, READ = (FORWARD + 6 + i for i in range(6))
    FLIP = READ + n_col - 1

    def halo_copy(t, side):
        return remote(
            state.at[t, :, own_ds[side]], halo_in[1 - side].at[t], 2 * t + side,
            {"elem": neighbour[side]},
        )

    def halo_across(side):
        return remote(
            state.at[STEPS, :, own_ds[side]], halo_in[1 - side].at[0], ACROSS,
            {"sec": other, "elem": neighbour[side]}, side,
        )

    def forward(side):
        return remote(
            state.at[STEPS, :, own_ds[side]], state.at[0, :, own_ds[side]],
            FORWARD + side, {"sec": other},
        )

    def out_copy(t, side):
        return remote(
            out[side].at[t], back[1 - side].at[t], 2 * STEPS + 2 * t + side,
            {"elem": neighbour[side]},
        )

    def out_across(side):
        return remote(
            out[side].at[last], back_across, RETURN, {"sec": other, "elem": neighbour[side]}
        )

    def backward(side):
        return remote(
            adjoint.at[STEPS, :, own_ds[side]], adjoint_in.at[:, own_ds[side]],
            BACKWARD + side, {"sec": other},
        )

    def half_copy(part, side):
        return remote(
            out_half.at[part], back_half, (LOWER, HIGHER)[part],
            {"sec": section if part == 0 else other, "elem": neighbour[side]},
        )

    def up(side):
        rows = pl.ds(own_elems[side].start, radius)
        return remote(upper.at[rows], upper_in.at[rows], UPPER + side, {"sec": other})

    @pl.when(section == 0)
    def _():
        halo_copy(0, LEFT).start()
        halo_copy(0, RIGHT).start()

    for e in range(elems):
        jac_loads[e].wait()

        def split_one(d, carry, e=e):
            target = lax.rem(first_elem + e + d - radius + elem_total, elem_total)
            slot = jnp.int32(0)
            for k in range(1, nbrs):
                slot = jnp.where(neighbors[e, k] == target, jnp.int32(k), slot)
            high, low = halves(jac_f32[e][slot])
            lanes = pl.ds(pl.multiple_of(d * order, order), order)
            jac_high[e][:, lanes] = high
            jac_low[e][:, lanes] = low
            return carry

        lax.fori_loop(0, nbrs, split_one, 0)

    weights_load.wait()
    weights_ref[stats:, :] = jnp.zeros((weights_ref.shape[0] - stats, order), F32)
    weights_high, weights_low = halves(weights_ref[...])
    lane_ids = lax.broadcasted_iota(jnp.int32, (cols, LANES), 1)
    station_row = jnp.full((cols, LANES), -1, jnp.int32)
    for i in range(stats):
        station_row = jnp.where(lane_ids == i, stations[i], station_row)

    def put_field(start, value):
        high, low = halves(value)
        field[:cols, start : start + value.shape[1]] = high
        field[cols:, start : start + value.shape[1]] = low

    def blocks(ref, begin, end):
        return ref[:, begin * order : end * order]

    def gathered(e, low, high):
        return product3(
            blocks(field, low, high), blocks(jac_high[e], low - e, high - e),
            blocks(jac_low[e], low - e, high - e), True,
        )

    def here(e):
        return slice(e * order, (e + 1) * order)

    def finish_tangent(t, side, away):
        halo_copy(t, 1 - side).wait_recv()
        put_field(0 if side == LEFT else width + full, halo_in[side][t])
        for e in own_elems[side]:
            span = (e, radius) if side == LEFT else (edge, e + nbrs)
            state[t + 1, :, here(e)] = state[t + 1, :, here(e)] + gathered(e, *span)
        if t < last:
            halo_copy(t + 1, side).start()
        else:

            @pl.when(section == 0)
            def _():
                forward(side).start()
                if away:
                    halo_across(side).start()

    def tangent(t, core, away):
        if t == 0:
            for side in (core, away):

                @pl.when(section == 1)
                def _():
                    forward(side).wait_recv()
                    if side == core:
                        halo_copy(0, core).start()

                put_field(width + own[side].start, state[0, :, own[side]])
                begin, end = own_span[side]
                for e in range(elems):
                    added = gathered(e, max(e, begin), min(e + nbrs, end))
                    if side == away:
                        added = added + (state[1, :, here(e)] + state[0, :, here(e)])
                    state[1, :, here(e)] = added
        finish_tangent(t, core, False)
        finish_tangent(t, away, True)

    for t in range(STEPS):
        if t > 0:
            put_field(width, state[t])
            for e in range(elems):
                added = gathered(e, max(e, radius), min(e + nbrs, edge))
                state[t + 1, :, here(e)] = state[t, :, here(e)] + added
        by_parity(functools.partial(tangent, t))

    reading = jnp.zeros((cols, LANES), F32)
    for e in range(elems):
        stack = jnp.concatenate(halves(state[STEPS, :, here(e)]), axis=0)
        read = product3(stack, weights_high, weights_low, True)
        read = jnp.where(station_row == first_elem + e, read, 0.0)
        reading = reading + read
        stack = jnp.concatenate(halves(read), axis=0)
        observed[:, here(e)] = product3(stack, weights_high, weights_low, False)
    for slot in range(n_col, readings.shape[0]):
        readings[slot] = jnp.zeros((cols, LANES), F32)
    readings[column] = reading
    read_copies = [
        remote(
            readings.at[column], readings.at[column], READ + j - 1,
            {"col": lax.rem(column + j, n_col)},
        )
        for j in range(1, n_col)
    ]
    for copy in read_copies:
        copy.start()
    gram_copy = remote(partial.at[rounds], partial_in.at[rounds], GRAM, {"sec": other})

    def project():
        for copy in read_copies:
            copy.wait_recv()
        everyone = readings[...].reshape(readings.shape[0] * cols, LANES)
        high, low = halves(everyone)
        stack = jnp.concatenate(halves(readings[column]), axis=0)
        partial[0] = product3(stack, high, low, True)
        for r in range(rounds):
            copy = remote(partial.at[r], partial_in.at[r], FLIP + r, flips[r])
            copy.start()
            copy.wait_recv()
            partial[r + 1] = partial[r] + partial_in[r]
            copy.wait_send()
        gram_copy.start()

    @pl.when(section == 0)
    def _():
        project()

    def spread(e, low, high):
        return product3(
            field[:, here(e)], blocks(jac_high[e], low - e, high - e),
            blocks(jac_low[e], low - e, high - e), False,
        )

    def send_out(t, side, away):
        put_field(own[side].start, adjoint[t, :, own[side]])
        ref = out[side]
        if side == LEFT:
            ref[t] = spread(0, 0, radius)
            for e in range(1, radius):
                ref[t, :, e * order :] = ref[t, :, e * order :] + spread(e, e, radius)
        else:
            ref[t] = spread(elems - 1, edge, edge + radius)
            for e in range(elems - radius, elems - 1):
                size = (e + nbrs - edge) * order
                ref[t, :, :size] = ref[t, :, :size] + spread(e, edge, e + nbrs)
        if t == last and away:

            @pl.when(section == 0)
            def _():
                for part in range(2):
                    for j in range(radius):
                        lanes = slice(j * order + part * half, j * order + (part + 1) * half)
                        out_half[part, :, j * half : (j + 1) * half] = ref[t, :, lanes]
                    half_copy(part, side).start()

            @pl.when(section == 1)
            def _():
                out_across(side).start()

        else:
            out_copy(t, side).start()

    def begin_adjoint(core, away):
        for side in (away, core):
            lanes = own[side]

            @pl.when(section == 0)
            def _():
                backward(side).wait_recv()
                total = adjoint_in[:, lanes] + observed[:, lanes]
                if side == away:
                    out_across(1 - side).wait_recv()
                    total = total + back_across[...]
                adjoint[0, :, lanes] = total

            @pl.when(section == 1)
            def _():
                adjoint[0, :, lanes] = observed[:, lanes]

            send_out(0, side, side == away)

    by_parity(begin_adjoint)

    def inner(t, side):
        begin, end = own_span[side]
        lanes = own[side]
        adjoint[t + 1, :, lanes] = adjoint[t, :, lanes]
        for e in range(elems):
            low, high = max(e, begin), min(e + nbrs, end)
            lanes = slice((low - radius) * order, (high - radius) * order)
            adjoint[t + 1, :, lanes] = adjoint[t + 1, :, lanes] + spread(e, low, high)

    def add_back(t, side):
        lanes = own[side]
        out_copy(t, 1 - side).wait_recv()
        adjoint[t + 1, :, lanes] = adjoint[t + 1, :, lanes] + back[side][t]

    def send_up(side):
        for e in own_elems[side]:
            upper[e] = adjoint[STEPS, :, e * order + half : (e + 1) * order]
        up(side).start()

    def lower_half(e):
        return adjoint[STEPS, :, e * order : e * order + half]

    def adjoint_step(t, core, away):
        if t < last:
            for side in (core, away):
                add_back(t, side)
                send_out(t + 1, side, side == away)
        else:
            inner(t, away)

            @pl.when(section == 0)
            def _():
                send_up(away)

            @pl.when(section == 1)
            def _():
                backward(away).start()

            inner(t, core)
            add_back(t, core)

            @pl.when(section == 0)
            def _():
                send_up(core)
                for e in own_elems[core]:
                    hess_ref[e] = lower_half(e)
                half_copy(0, 1 - away).wait_recv()
                for j, e in enumerate(own_elems[away]):
                    hess_ref[e] = lower_half(e) + back_half[:, j * half : (j + 1) * half]

            @pl.when(section == 1)
            def _():
                backward(core).start()

    for t in range(STEPS):
        if t < last:
            inner(t, LEFT)
            inner(t, RIGHT)
        by_parity(functools.partial(adjoint_step, t))

    @pl.when(section == 1)
    def _():
        project()

    gram_copy.wait_recv()
    scale = 1.0 / (elem_total * order)
    gram_ref[...] = (partial[rounds] + partial_in[rounds]) * scale

    def close(core, away):
        for t in range(STEPS):
            for side in (core, away):

                @pl.when((section == 0) | (t > 0) | (side == core))
                def _():
                    halo_copy(t, side).wait_send()

                if t < last or side == core:
                    out_copy(t, side).wait_send()

        @pl.when(section == 0)
        def _():
            halo_across(away).wait_send()
            for side in (core, away):
                forward(side).wait_send()
                up(side).wait_send()
            for part in range(2):
                half_copy(part, away).wait_send()

        @pl.when(section == 1)
        def _():
            out_across(away).wait_send()
            for side in (core, away):
                backward(side).wait_send()
                up(side).wait_recv()
            for e in own_elems[core]:
                hess_ref[e] = upper_in[e]
            half_copy(1, 1 - away).wait_recv()
            for j, e in enumerate(own_elems[away]):
                hess_ref[e] = upper_in[e] + back_half[:, j * half : (j + 1) * half]

    by_parity(close)
    gram_copy.wait_send()
    for copy in read_copies:
        copy.wait_send()


def hand_over(hess_ref, gram_ref, hess_out, gram_out):
    hess_out[...] = hess_ref[...]
    gram_out[...] = gram_ref[:, : gram_out.shape[1]]


def per_device(n_elem, n_col, probes, jacobian, neighbors, stations, obs_weights):
    cols, elems, order = probes.shape
    nbrs = neighbors.shape[1]
    stats = stations.shape[0]
    radius = (nbrs - 1) // 2
    rounds = int(math.log2(n_elem))
    slots = max(n_col, LANES // cols)
    sizes = (cols, elems, order, nbrs, stats, n_elem, n_col)
    full, width = elems * order, radius * order
    copies = 4 * STEPS + 11 + (n_col - 1) + rounds
    scratch = [pltpu.VMEM((nbrs, order, order), F32)] * elems
    scratch += [pltpu.VMEM((order, nbrs * order), BF16)] * (2 * elems)
    scratch += [
        pltpu.VMEM((elems, cols, order), F32),
        pltpu.VMEM((LANES, order), F32),
        pltpu.VMEM((STEPS + 1, cols, full), F32),
        pltpu.VMEM((2 * cols, full + 2 * width), BF16),
        pltpu.VMEM((STEPS, cols, width), F32),
        pltpu.VMEM((STEPS, cols, width), F32),
        pltpu.VMEM((STEPS + 1, cols, full), F32),
        pltpu.VMEM((cols, full), F32),
        pltpu.VMEM((cols, full), F32),
        pltpu.VMEM((STEPS, cols, width), F32),
        pltpu.VMEM((STEPS, cols, width), F32),
        pltpu.VMEM((STEPS, cols, width), F32),
        pltpu.VMEM((STEPS, cols, width), F32),
        pltpu.VMEM((cols, width), F32),
        pltpu.VMEM((2, cols, width // 2), F32),
        pltpu.VMEM((cols, width // 2), F32),
        pltpu.VMEM((slots, cols, LANES), F32),
        pltpu.VMEM((rounds + 1, cols, slots * cols), F32),
        pltpu.VMEM((rounds + 1, cols, slots * cols), F32),
        pltpu.VMEM((elems, cols, order // 2), F32),
        pltpu.VMEM((elems, cols, order // 2), F32),
        pltpu.SemaphoreType.DMA((elems + 2,)),
        pltpu.SemaphoreType.DMA((copies,)),
        pltpu.SemaphoreType.DMA((copies,)),
    ]
    smem = pl.BlockSpec(memory_space=pltpu.SMEM)
    anywhere = pl.BlockSpec(memory_space=pl.ANY)
    vmem = pl.BlockSpec(memory_space=pltpu.VMEM)
    hess, gram = pl.pallas_call(
        functools.partial(kernel, sizes),
        out_shape=(
            jax.ShapeDtypeStruct((elems, cols, order // 2), F32),
            jax.ShapeDtypeStruct((cols, slots * cols), F32),
        ),
        in_specs=[smem, smem, anywhere, anywhere, anywhere],
        out_specs=(vmem, vmem),
        scratch_shapes=scratch,
        compiler_params=pltpu.CompilerParams(
            collective_id=0, has_side_effects=True, vmem_limit_bytes=56 * 1024 * 1024
        ),
    )(neighbors, stations, probes.transpose(1, 0, 2), jacobian, obs_weights)
    hess, gram = pl.pallas_call(
        hand_over,
        out_shape=(
            jax.ShapeDtypeStruct(hess.shape, F32),
            jax.ShapeDtypeStruct((cols, n_col * cols), F32),
        ),
        in_specs=[vmem, vmem],
        out_specs=(vmem, vmem),
    )(hess, gram)
    return hess.transpose(1, 0, 2), gram


def solution(mesh):
    in_specs = (
        P("col", "elem", None),
        P("sec", "elem", None, None, None),
        P("elem", None),
        P("elem"),
        P("elem", None),
    )
    out_specs = (P("col", "elem", "sec"), P("col", None))
    body = functools.partial(per_device, mesh.shape["elem"], mesh.shape["col"])
    return jax.shard_map(
        body, mesh=mesh, in_specs=in_specs, out_specs=out_specs, check_vma=False
    )
```

profile of v0, /device:TPU:0, one launch (start us, length us, event | category | flops | bytes accessed | tf_op | source)
XLA Modules:
  0.0 56.5 jit_solution(10026493238071927582)
XLA Ops:
  0.6 54.3 %shard_map.68 = (f32[6,32,128]{2,1,0:T(8,128)}, f32[32,128]{1,0:T(8,128)}) custom-call(s32[6,7]{1,0:T(8,128)} %neighbors.1, s32[64]{0:T(128)} %stations.1, f32[6,32,256]{2,1,0:T(8,128)} %bitcast.2, f32[1,6,7,256,256]{4,3,2,1,0:T(8,128)} %jacobian_hbm.1, f32[64,256]{1,0:T(8,128)} %weights_hbm.1), custom_call_target="tpu_custom_call" | custom-call | tf_op jit(solution)/shard_map/pallas_call | solution.py:522
  55.0 1.5 %shard_map.69 = (f32[6,32,128]{2,1,0:T(8,128)}, f32[32,64]{1,0:T(8,128)}) custom-call(f32[6,32,128]{2,1,0:T(8,128)} %get-tuple-element.6.hess_ref, f32[32,128]{1,0:T(8,128)} %get-tuple-element.7.gram_ref), custom_call_target="tpu_custom_call" | custom-call | tf_op jit(solution)/shard_map/pallas_call | solution.py:535
where the time goes:
time: 56.7 us; the launch traced here: 56.5 us
  Pallas kernels  55.9 us (99%)
  between operations  0.64 us (1%)
    pallas_call x1, Pallas kernels, per_device(): pl.pallas_call(functools.partial(kernel, sizes), out_shape=(jax.ShapeDtyp...  54.3 us
    pallas_call x1, Pallas kernels, per_device(): pl.pallas_call(hand_over, out_shape=(jax.ShapeDtypeStruct(hess.shape, F32...  1.55 us

commit v1 on v0

--- a/solution.py
+++ b/solution.py
@@ -48,6 +48,7 @@
     radius = (nbrs - 1) // 2
     width = radius * order
     half = order // 2
+    seats = LANES // 2
     jac_f32 = scratch[:elems]
     jac_high = scratch[elems : 2 * elems]
     jac_low = scratch[2 * elems : 3 * elems]
@@ -55,6 +56,8 @@
         probes_ref, weights_ref, state, field, halo_left, halo_right,
         adjoint, adjoint_in, observed, out_left, out_right, back_left, back_right,
         back_across, out_half, back_half, readings, partial, partial_in, upper, upper_in,
+        u_high, u_low, placed_field, once, once_field, once_halo, once_left, once_right,
+        answer_out, answer_in,
         load_sem, send_sem, recv_sem,
     ) = scratch[3 * elems :]
     section = lax.axis_index("sec")
@@ -76,6 +79,7 @@
     halo_in = (halo_left, halo_right)
     out = (out_left, out_right)
     back = (back_left, back_right)
+    once_in = (once_left, once_right)
     own = (slice(0, width), slice(full - width, full))
     own_ds = (pl.ds(0, width), pl.ds(full - width, width))
     own_elems = (range(0, radius), range(elems - radius, elems))
@@ -111,6 +115,9 @@
         bit = 1 << r
         upper_bit = lax.rem(block // bit, 2)
         flips.append({"elem": block + bit - 2 * bit * upper_bit})
+    second_left = lax.rem(block + n_elem - 2, n_elem)
+    second_right = lax.rem(block + 2, n_elem)
+    partners += [{"elem": second_left}, {"elem": second_right}]
     for partner in partners + flips:
         pl.semaphore_signal(barrier, inc=1, device_id=partner, device_id_type=MESH)
 
@@ -134,6 +141,8 @@
     BACKWARD, UPPER = FORWARD + 2, FORWARD + 4
     ACROSS, RETURN, GRAM, LOWER, HIGHER, READ = (FORWARD + 6 + i for i in range(6))
     FLIP = READ + n_col - 1
+    ONCE = FLIP + rounds
+    ANSWER = ONCE + 2
 
     def halo_copy(t, side):
         return remote(
@@ -163,6 +172,20 @@
         return remote(
             out[side].at[last], back_across, RETURN, {"sec": other, "elem": neighbour[side]}
         )
+
+    def once_copy(side):
+        start = 0 if side == LEFT else width + full
+        return remote(
+            once.at[:, pl.ds(start, width)], once_in[1 - side], ONCE + side,
+            {"elem": neighbour[side]},
+        )
+
+    answer_copies = [
+        remote(answer_out.at[part], answer_in.at[slot], ANSWER + slot, {"elem": target})
+        for slot, (part, target) in enumerate(
+            ((1, right), (1, second_right), (0, left), (0, second_left))
+        )
+    ]
 
     def backward(side):
         return remote(
@@ -235,52 +258,159 @@
         if t < last:
             halo_copy(t + 1, side).start()
         else:
-
-            @pl.when(section == 0)
-            def _():
-                forward(side).start()
-                if away:
-                    halo_across(side).start()
+            forward(side).start()
+            if away:
+                halo_across(side).start()
 
     def tangent(t, core, away):
-        if t == 0:
-            for side in (core, away):
-
-                @pl.when(section == 1)
-                def _():
-                    forward(side).wait_recv()
-                    if side == core:
-                        halo_copy(0, core).start()
-
-                put_field(width + own[side].start, state[0, :, own[side]])
-                begin, end = own_span[side]
-                for e in range(elems):
-                    added = gathered(e, max(e, begin), min(e + nbrs, end))
-                    if side == away:
-                        added = added + (state[1, :, here(e)] + state[0, :, here(e)])
-                    state[1, :, here(e)] = added
         finish_tangent(t, core, False)
         finish_tangent(t, away, True)
 
-    for t in range(STEPS):
-        if t > 0:
+    @pl.when(section == 0)
+    def _():
+        for t in range(STEPS):
             put_field(width, state[t])
             for e in range(elems):
                 added = gathered(e, max(e, radius), min(e + nbrs, edge))
                 state[t + 1, :, here(e)] = state[t, :, here(e)] + added
-        by_parity(functools.partial(tangent, t))
-
-    reading = jnp.zeros((cols, LANES), F32)
-    for e in range(elems):
-        stack = jnp.concatenate(halves(state[STEPS, :, here(e)]), axis=0)
-        read = product3(stack, weights_high, weights_low, True)
-        read = jnp.where(station_row == first_elem + e, read, 0.0)
-        reading = reading + read
-        stack = jnp.concatenate(halves(read), axis=0)
-        observed[:, here(e)] = product3(stack, weights_high, weights_low, False)
+            by_parity(functools.partial(tangent, t))
+
+    def by_block(source, rows, elements, m):
+        first, second = None, None
+        for e in elements:
+            if abs(m - e) > radius:
+                continue
+            low = m - e + radius
+            up_term = product(source[:, here(e)], blocks(jac_high[e], low, low + 1), False)
+            low_term = product(source[:rows, here(e)], blocks(jac_low[e], low, low + 1), False)
+            first = up_term if first is None else first + up_term
+            second = low_term if second is None else second + low_term
+        return first[:rows] + (first[rows:] + second)
+
+    def there(m):
+        return slice((m + radius) * order, (m + radius + 1) * order)
+
+    def put_rows(start, m, value):
+        high, low = halves(value)
+        u_high[start : start + seats, there(m)] = high
+        u_low[start : start + seats, there(m)] = low
+
+    def station_products():
+        u_high[...] = jnp.zeros(u_high.shape, BF16)
+        u_low[...] = jnp.zeros(u_low.shape, BF16)
+        row_ids = lax.broadcasted_iota(jnp.int32, (seats, order), 0)
+        station_col = jnp.full((seats, order), -1, jnp.int32)
+        for i in range(stats):
+            station_col = jnp.where(row_ids == i, stations[i], station_col)
+
+        def placed(e):
+            return jnp.where(station_col == first_elem + e, weights_ref[:seats, :], 0.0)
+
+        for e in range(elems):
+            high, low = halves(placed(e))
+            placed_field[:seats, here(e)] = high
+            placed_field[seats:, here(e)] = low
+        for side, span in ((LEFT, range(-radius, 0)), (RIGHT, range(elems, elems + radius))):
+            for m in span:
+                once[:, there(m)] = by_block(placed_field, seats, range(elems), m)
+            once_copy(side).start()
+        for m in range(elems):
+            value = by_block(placed_field, seats, range(elems), m) + placed(m)
+            once[:, there(m)] = value
+            high, low = halves(value)
+            once_field[:seats, here(m)] = high
+            once_field[seats:, here(m)] = low
+        for m in range(-radius, elems + radius):
+            value = by_block(once_field, seats, range(elems), m)
+            if 0 <= m < elems:
+                value = value + once[:, there(m)]
+            put_rows(seats, m, value)
+        for side in (LEFT, RIGHT):
+            once_copy(1 - side).wait_recv()
+            high, low = halves(once_in[side][...])
+            once_halo[:seats, own[side]] = high
+            once_halo[seats:, own[side]] = low
+            reach = own_elems[side]
+            for m in range(reach.start - radius, reach.stop + radius):
+                value = by_block(once_halo, seats, reach, m)
+                if m in reach:
+                    j = (m - reach.start) * order
+                    value = value + once_in[side][:, j : j + order]
+                put_rows(0 if side == LEFT else 3 * seats, m, value)
+
+    def lanes_of(side, halo):
+        if halo:
+            start = 0 if side == LEFT else width + full
+        else:
+            start = width + own[side].start
+        return slice(start, start + width)
+
+    def answered(lanes):
+        return product3(field[:, lanes], u_high[:, lanes], u_low[:, lanes], True)
+
+    def respond(core, away):
+        total = None
+        for side in (core, away):
+            forward(side).wait_recv()
+            if side == core:
+                halo_copy(0, core).start()
+            put_field(width + own[side].start, state[0, :, own[side]])
+            part = answered(lanes_of(side, False))
+            total = part if total is None else total + part
+            halo_copy(0, 1 - side).wait_recv()
+            put_field(lanes_of(side, True).start, halo_in[side][0])
+            total = total + answered(lanes_of(side, True))
+        near = lane_ids < seats
+        to_left = total[:, :LANES]
+        to_right = total[:, LANES:] + jnp.where(near, pltpu.roll(to_left, seats, 1), 0.0)
+        answer_out[0] = to_left
+        answer_out[1] = to_right
+        for copy in answer_copies:
+            copy.start()
+        for copy in answer_copies:
+            copy.wait_recv()
+        from_left, beyond_left = answer_in[0], answer_in[1]
+        from_right, beyond_right = answer_in[2], answer_in[3]
+        upper_half = from_left + to_left
+        upper_half = upper_half + pltpu.roll(jnp.where(near, from_right, beyond_left), seats, 1)
+        lower = from_right + to_right
+        lower = lower + pltpu.roll(jnp.where(near, beyond_right, from_left), seats, 1)
+        stack = jnp.concatenate(halves(jnp.concatenate([upper_half, lower], axis=1)), axis=0)
+
+        def returned(lanes):
+            return product3(stack, u_high[:, lanes], u_low[:, lanes], False)
+
+        out[away][last] = returned(lanes_of(away, True))
+        out_across(away).start()
+        adjoint[STEPS, :, own[away]] = returned(lanes_of(away, False))
+        backward(away).start()
+        out[core][0] = returned(lanes_of(core, True))
+        out_copy(0, core).start()
+        value = returned(lanes_of(core, False))
+        out_copy(0, 1 - core).wait_recv()
+        adjoint[STEPS, :, own[core]] = value + back[core][0]
+        backward(core).start()
+        readings[column] = jnp.where(near, lower, 0.0)
+
+    @pl.when(section == 1)
+    def _():
+        station_products()
+        by_parity(respond)
+
+    @pl.when(section == 0)
+    def _():
+        reading = jnp.zeros((cols, LANES), F32)
+        for e in range(elems):
+            stack = jnp.concatenate(halves(state[STEPS, :, here(e)]), axis=0)
+            read = product3(stack, weights_high, weights_low, True)
+            read = jnp.where(station_row == first_elem + e, read, 0.0)
+            reading = reading + read
+            stack = jnp.concatenate(halves(read), axis=0)
+            observed[:, here(e)] = product3(stack, weights_high, weights_low, False)
+        readings[column] = reading
+
     for slot in range(n_col, readings.shape[0]):
         readings[slot] = jnp.zeros((cols, LANES), F32)
-    readings[column] = reading
     read_copies = [
         remote(
             readings.at[column], readings.at[column], READ + j - 1,
@@ -307,9 +437,7 @@
             copy.wait_send()
         gram_copy.start()
 
-    @pl.when(section == 0)
-    def _():
-        project()
+    project()
 
     def spread(e, low, high):
         return product3(
@@ -330,42 +458,24 @@
                 size = (e + nbrs - edge) * order
                 ref[t, :, :size] = ref[t, :, :size] + spread(e, edge, e + nbrs)
         if t == last and away:
-
-            @pl.when(section == 0)
-            def _():
-                for part in range(2):
-                    for j in range(radius):
-                        lanes = slice(j * order + part * half, j * order + (part + 1) * half)
-                        out_half[part, :, j * half : (j + 1) * half] = ref[t, :, lanes]
-                    half_copy(part, side).start()
-
-            @pl.when(section == 1)
-            def _():
-                out_across(side).start()
-
+            for part in range(2):
+                for j in range(radius):
+                    lanes = slice(j * order + part * half, j * order + (part + 1) * half)
+                    out_half[part, :, j * half : (j + 1) * half] = ref[t, :, lanes]
+                half_copy(part, side).start()
         else:
             out_copy(t, side).start()
 
     def begin_adjoint(core, away):
         for side in (away, core):
             lanes = own[side]
-
-            @pl.when(section == 0)
-            def _():
-                backward(side).wait_recv()
-                total = adjoint_in[:, lanes] + observed[:, lanes]
-                if side == away:
-                    out_across(1 - side).wait_recv()
-                    total = total + back_across[...]
-                adjoint[0, :, lanes] = total
-
-            @pl.when(section == 1)
-            def _():
-                adjoint[0, :, lanes] = observed[:, lanes]
-
+            backward(side).wait_recv()
+            total = adjoint_in[:, lanes] + observed[:, lanes]
+            if side == away:
+                out_across(1 - side).wait_recv()
+                total = total + back_across[...]
+            adjoint[0, :, lanes] = total
             send_out(0, side, side == away)
-
-    by_parity(begin_adjoint)
 
     def inner(t, side):
         begin, end = own_span[side]
@@ -396,58 +506,37 @@
                 send_out(t + 1, side, side == away)
         else:
             inner(t, away)
-
-            @pl.when(section == 0)
-            def _():
-                send_up(away)
-
-            @pl.when(section == 1)
-            def _():
-                backward(away).start()
-
+            send_up(away)
             inner(t, core)
             add_back(t, core)
-
-            @pl.when(section == 0)
-            def _():
-                send_up(core)
-                for e in own_elems[core]:
-                    hess_ref[e] = lower_half(e)
-                half_copy(0, 1 - away).wait_recv()
-                for j, e in enumerate(own_elems[away]):
-                    hess_ref[e] = lower_half(e) + back_half[:, j * half : (j + 1) * half]
-
-            @pl.when(section == 1)
-            def _():
-                backward(core).start()
-
-    for t in range(STEPS):
-        if t < last:
-            inner(t, LEFT)
-            inner(t, RIGHT)
-        by_parity(functools.partial(adjoint_step, t))
-
-    @pl.when(section == 1)
+            send_up(core)
+            for e in own_elems[core]:
+                hess_ref[e] = lower_half(e)
+            half_copy(0, 1 - away).wait_recv()
+            for j, e in enumerate(own_elems[away]):
+                hess_ref[e] = lower_half(e) + back_half[:, j * half : (j + 1) * half]
+
+    @pl.when(section == 0)
     def _():
-        project()
+        by_parity(begin_adjoint)
+        for t in range(STEPS):
+            if t < last:
+                inner(t, LEFT)
+                inner(t, RIGHT)
+            by_parity(functools.partial(adjoint_step, t))
 
     gram_copy.wait_recv()
     scale = 1.0 / (elem_total * order)
     gram_ref[...] = (partial[rounds] + partial_in[rounds]) * scale
 
     def close(core, away):
-        for t in range(STEPS):
-            for side in (core, away):
-
-                @pl.when((section == 0) | (t > 0) | (side == core))
-                def _():
-                    halo_copy(t, side).wait_send()
-
-                if t < last or side == core:
-                    out_copy(t, side).wait_send()
-
         @pl.when(section == 0)
         def _():
+            for t in range(STEPS):
+                for side in (core, away):
+                    halo_copy(t, side).wait_send()
+                    if t < last or side == core:
+                        out_copy(t, side).wait_send()
             halo_across(away).wait_send()
             for side in (core, away):
                 forward(side).wait_send()
@@ -457,8 +546,13 @@
 
         @pl.when(section == 1)
         def _():
+            halo_copy(0, core).wait_send()
+            out_copy(0, core).wait_send()
             out_across(away).wait_send()
+            for copy in answer_copies:
+                copy.wait_send()
             for side in (core, away):
+                once_copy(side).wait_send()
                 backward(side).wait_send()
                 up(side).wait_recv()
             for e in own_elems[core]:
@@ -487,7 +581,8 @@
     slots = max(n_col, LANES // cols)
     sizes = (cols, elems, order, nbrs, stats, n_elem, n_col)
     full, width = elems * order, radius * order
-    copies = 4 * STEPS + 11 + (n_col - 1) + rounds
+    copies = 4 * STEPS + 17 + (n_col - 1) + rounds
+    seats = LANES // 2
     scratch = [pltpu.VMEM((nbrs, order, order), F32)] * elems
     scratch += [pltpu.VMEM((order, nbrs * order), BF16)] * (2 * elems)
     scratch += [
@@ -512,6 +607,16 @@
         pltpu.VMEM((rounds + 1, cols, slots * cols), F32),
         pltpu.VMEM((elems, cols, order // 2), F32),
         pltpu.VMEM((elems, cols, order // 2), F32),
+        pltpu.VMEM((4 * seats, full + 2 * width), BF16),
+        pltpu.VMEM((4 * seats, full + 2 * width), BF16),
+        pltpu.VMEM((2 * seats, full), BF16),
+        pltpu.VMEM((seats, full + 2 * width), F32),
+        pltpu.VMEM((2 * seats, full), BF16),
+        pltpu.VMEM((2 * seats, full), BF16),
+        pltpu.VMEM((seats, width), F32),
+        pltpu.VMEM((seats, width), F32),
+        pltpu.VMEM((2, cols, LANES), F32),
+        pltpu.VMEM((4, cols, LANES), F32),
         pltpu.SemaphoreType.DMA((elems + 2,)),
         pltpu.SemaphoreType.DMA((copies,)),
         pltpu.SemaphoreType.DMA((copies,)),

time: 56.7 us -> 48.1 us (0.85)
  Pallas kernels: 55.9 us -> 47.2 us
    pallas_call x1, Pallas kernels: 54.3 us -> 45.7 us  [per_device(): pl.pallas_call(functools.partial(kernel, sizes), out_shape=(jax.ShapeDtyp...]
where the time goes in v1:
time: 48.1 us; the launch traced here: 47.9 us
  Pallas kernels  47.2 us (98%)
  between operations  0.64 us (1%)
    pallas_call x1, Pallas kernels, per_device(): pl.pallas_call(functools.partial(kernel, sizes), out_shape=(jax.ShapeDtyp...  45.7 us
    pallas_call x1, Pallas kernels, per_device(): pl.pallas_call(hand_over, out_shape=(jax.ShapeDtypeStruct(hess.shape, F32...  1.55 us

profile of v1, /device:TPU:0, one launch (start us, length us, event | category | flops | bytes accessed | tf_op | source)
XLA Modules:
  0.0 47.9 jit_solution(190731017944429890)
XLA Ops:
  0.6 45.7 %shard_map.68 = (f32[6,32,128]{2,1,0:T(8,128)}, f32[32,128]{1,0:T(8,128)}) custom-call(s32[6,7]{1,0:T(8,128)} %neighbors.1, s32[64]{0:T(128)} %stations.1, f32[6,32,256]{2,1,0:T(8,128)} %bitcast.2, f32[1,6,7,256,256]{4,3,2,1,0:T(8,128)} %jacobian_hbm.1, f32[64,256]{1,0:T(8,128)} %weights_hbm.1), custom_call_target="tpu_custom_call" | custom-call | tf_op jit(solution)/shard_map/pallas_call | solution.py:627
  46.3 1.5 %shard_map.69 = (f32[6,32,128]{2,1,0:T(8,128)}, f32[32,64]{1,0:T(8,128)}) custom-call(f32[6,32,128]{2,1,0:T(8,128)} %get-tuple-element.6.hess_ref, f32[32,128]{1,0:T(8,128)} %get-tuple-element.7.gram_ref), custom_call_target="tpu_custom_call" | custom-call | tf_op jit(solution)/shard_map/pallas_call | solution.py:640

commit v2 on v1

--- a/solution.py
+++ b/solution.py
@@ -35,8 +35,8 @@
 
 def kernel(
     sizes,
-    neighbors,
-    stations,
+    neighbors_hbm,
+    stations_hbm,
     probes_hbm,
     jacobian_hbm,
     weights_hbm,
@@ -55,9 +55,10 @@
     (
         probes_ref, weights_ref, state, field, halo_left, halo_right,
         adjoint, adjoint_in, observed, out_left, out_right, back_left, back_right,
-        back_across, out_half, back_half, readings, partial, partial_in, upper, upper_in,
+        out_half, back_half, readings, partial, partial_in, upper, upper_in,
         u_high, u_low, placed_field, once, once_field, once_halo, once_left, once_right,
-        answer_out, answer_in,
+        spill_left, spill_right, spill_in_left, spill_in_right,
+        answer_out, answer_in, neighbors, stations,
         load_sem, send_sem, recv_sem,
     ) = scratch[3 * elems :]
     section = lax.axis_index("sec")
@@ -80,6 +81,10 @@
     out = (out_left, out_right)
     back = (back_left, back_right)
     once_in = (once_left, once_right)
+    spill = (spill_left, spill_right)
+    spill_in = (spill_in_left, spill_in_right)
+    own_rows = (slice(seats, 2 * seats), slice(0, seats))
+    other_rows = (slice(0, seats), slice(seats, 2 * seats))
     own = (slice(0, width), slice(full - width, full))
     own_ds = (pl.ds(0, width), pl.ds(full - width, width))
     own_elems = (range(0, radius), range(elems - radius, elems))
@@ -96,16 +101,22 @@
 
     probe_load = pltpu.make_async_copy(probes_hbm, probes_ref, load_sem.at[elems])
     probe_load.start()
+    table_loads = [
+        pltpu.make_async_copy(neighbors_hbm, neighbors, load_sem.at[elems + 2]),
+        pltpu.make_async_copy(stations_hbm, stations, load_sem.at[elems + 3]),
+    ]
+    for load in table_loads:
+        load.start()
+    weights_load = pltpu.make_async_copy(
+        weights_hbm, weights_ref.at[pl.ds(0, stats)], load_sem.at[elems + 1]
+    )
+    weights_load.start()
     jac_loads = [
         pltpu.make_async_copy(jacobian_hbm.at[0, e], jac_f32[e], load_sem.at[e])
         for e in range(elems)
     ]
     for load in jac_loads:
         load.start()
-    weights_load = pltpu.make_async_copy(
-        weights_hbm, weights_ref.at[pl.ds(0, stats)], load_sem.at[elems + 1]
-    )
-    weights_load.start()
 
     barrier = pltpu.get_barrier_semaphore()
     partners = [{"elem": left}, {"elem": right}, {"sec": other}, {"sec": other, "elem": far}]
@@ -139,10 +150,11 @@
 
     FORWARD = 4 * STEPS
     BACKWARD, UPPER = FORWARD + 2, FORWARD + 4
-    ACROSS, RETURN, GRAM, LOWER, HIGHER, READ = (FORWARD + 6 + i for i in range(6))
+    ACROSS, GRAM, LOWER, HIGHER, READ = (FORWARD + 6 + i for i in range(5))
     FLIP = READ + n_col - 1
     ONCE = FLIP + rounds
     ANSWER = ONCE + 2
+    SPILL = ANSWER + 4
 
     def halo_copy(t, side):
         return remote(
@@ -168,9 +180,12 @@
             {"elem": neighbour[side]},
         )
 
-    def out_across(side):
+    def spill_copy(side, first):
+        rows = own_rows[side] if first else other_rows[side]
+        rows = pl.ds(rows.start, seats)
         return remote(
-            out[side].at[last], back_across, RETURN, {"sec": other, "elem": neighbour[side]}
+            spill[side].at[rows], spill_in[1 - side].at[rows], SPILL + 2 * side + int(first),
+            {"elem": neighbour[side]},
         )
 
     def once_copy(side):
@@ -208,29 +223,26 @@
         halo_copy(0, LEFT).start()
         halo_copy(0, RIGHT).start()
 
-    for e in range(elems):
-        jac_loads[e].wait()
-
-        def split_one(d, carry, e=e):
+    for load in table_loads:
+        load.wait()
+
+    def split(e, use):
+        for d in range(nbrs):
             target = lax.rem(first_elem + e + d - radius + elem_total, elem_total)
             slot = jnp.int32(0)
             for k in range(1, nbrs):
                 slot = jnp.where(neighbors[e, k] == target, jnp.int32(k), slot)
             high, low = halves(jac_f32[e][slot])
-            lanes = pl.ds(pl.multiple_of(d * order, order), order)
-            jac_high[e][:, lanes] = high
-            jac_low[e][:, lanes] = low
-            return carry
-
-        lax.fori_loop(0, nbrs, split_one, 0)
-
-    weights_load.wait()
-    weights_ref[stats:, :] = jnp.zeros((weights_ref.shape[0] - stats, order), F32)
-    weights_high, weights_low = halves(weights_ref[...])
+            jac_high[e][:, d * order : (d + 1) * order] = high
+            jac_low[e][:, d * order : (d + 1) * order] = low
+            use(e + d - radius, high, low)
+
     lane_ids = lax.broadcasted_iota(jnp.int32, (cols, LANES), 1)
-    station_row = jnp.full((cols, LANES), -1, jnp.int32)
-    for i in range(stats):
-        station_row = jnp.where(lane_ids == i, stations[i], station_row)
+
+    def take_weights():
+        weights_load.wait()
+        if weights_ref.shape[0] > stats:
+            weights_ref[stats:, :] = jnp.zeros((weights_ref.shape[0] - stats, order), F32)
 
     def put_field(start, value):
         high, low = halves(value)
@@ -248,6 +260,10 @@
 
     def here(e):
         return slice(e * order, (e + 1) * order)
+
+    def advance(t, e):
+        added = gathered(e, max(e, radius), min(e + nbrs, edge))
+        state[t + 1, :, here(e)] = state[t, :, here(e)] + added
 
     def finish_tangent(t, side, away):
         halo_copy(t, 1 - side).wait_recv()
@@ -263,16 +279,32 @@
                 halo_across(side).start()
 
     def tangent(t, core, away):
-        finish_tangent(t, core, False)
-        finish_tangent(t, away, True)
+        if t > 0:
+            put_field(width, state[t])
+        for side in (away, core) if t == 0 else (core, away):
+            if t > 0:
+                for e in own_elems[side]:
+                    advance(t, e)
+            finish_tangent(t, side, side == away)
 
     @pl.when(section == 0)
     def _():
+        put_field(width, state[0])
+        for e in range(elems):
+            jac_loads[e].wait()
+            terms = [None, None]
+
+            def use(m, high, low):
+                if 0 <= m < elems:
+                    source = blocks(field, m + radius, m + radius + 1)
+                    pair = product(source, high, True), product(source[:cols], low, True)
+                    for i in range(2):
+                        terms[i] = pair[i] if terms[i] is None else terms[i] + pair[i]
+
+            split(e, use)
+            added = terms[0][:cols] + (terms[0][cols:] + terms[1])
+            state[1, :, here(e)] = state[0, :, here(e)] + added
         for t in range(STEPS):
-            put_field(width, state[t])
-            for e in range(elems):
-                added = gathered(e, max(e, radius), min(e + nbrs, edge))
-                state[t + 1, :, here(e)] = state[t, :, here(e)] + added
             by_parity(functools.partial(tangent, t))
 
     def by_block(source, rows, elements, m):
@@ -296,6 +328,7 @@
         u_low[start : start + seats, there(m)] = low
 
     def station_products():
+        take_weights()
         u_high[...] = jnp.zeros(u_high.shape, BF16)
         u_low[...] = jnp.zeros(u_low.shape, BF16)
         row_ids = lax.broadcasted_iota(jnp.int32, (seats, order), 0)
@@ -310,33 +343,68 @@
             high, low = halves(placed(e))
             placed_field[:seats, here(e)] = high
             placed_field[seats:, here(e)] = low
-        for side, span in ((LEFT, range(-radius, 0)), (RIGHT, range(elems, elems + radius))):
-            for m in span:
-                once[:, there(m)] = by_block(placed_field, seats, range(elems), m)
-            once_copy(side).start()
+
+        for e in range(elems):
+            jac_loads[e].wait()
+
+            def use(m, high, low, e=e):
+                source = placed_field[:, here(e)]
+                first = product(source, high, False)
+                value = first[seats:] + product(source[:seats], low, False)
+                value = first[:seats] + value
+                if m == e:
+                    value = value + placed(e)
+                if e > 0 and m < e + radius:
+                    value = value + once[:, there(m)]
+                once[:, there(m)] = value
+
+            split(e, use)
+            if e == radius - 1:
+                once_copy(LEFT).start()
+        once_copy(RIGHT).start()
         for m in range(elems):
-            value = by_block(placed_field, seats, range(elems), m) + placed(m)
-            once[:, there(m)] = value
-            high, low = halves(value)
+            high, low = halves(once[:, there(m)])
             once_field[:seats, here(m)] = high
             once_field[seats:, here(m)] = low
-        for m in range(-radius, elems + radius):
+        for side, span in ((LEFT, range(-radius, 0)), (RIGHT, range(elems, elems + radius))):
+            for j, m in enumerate(span):
+                value = by_block(once_field, seats, range(elems), m)
+                put_rows(seats, m, value)
+                spill[side][own_rows[side], here(j)] = value
+            spill_copy(side, True).start()
+        for m in range(elems):
             value = by_block(once_field, seats, range(elems), m)
-            if 0 <= m < elems:
-                value = value + once[:, there(m)]
-            put_rows(seats, m, value)
+            put_rows(seats, m, value + once[:, there(m)])
         for side in (LEFT, RIGHT):
             once_copy(1 - side).wait_recv()
             high, low = halves(once_in[side][...])
             once_halo[:seats, own[side]] = high
             once_halo[seats:, own[side]] = low
             reach = own_elems[side]
-            for m in range(reach.start - radius, reach.stop + radius):
+            outside = range(-radius, 0) if side == LEFT else range(elems, elems + radius)
+            for j, m in enumerate(outside):
+                value = by_block(once_halo, seats, reach, m)
+                put_rows(0 if side == LEFT else 3 * seats, m, value)
+                spill[side][other_rows[side], here(j)] = value
+            spill_copy(side, False).start()
+            for m in range(elems):
+                if m - reach.stop >= radius or reach.start - m > radius:
+                    continue
                 value = by_block(once_halo, seats, reach, m)
                 if m in reach:
-                    j = (m - reach.start) * order
-                    value = value + once_in[side][:, j : j + order]
+                    value = value + once_in[side][:, here(m - reach.start)]
                 put_rows(0 if side == LEFT else 3 * seats, m, value)
+
+    def merge(side):
+        for part in (True, False):
+            spill_copy(1 - side, part).wait_recv()
+        starts = (0, seats) if side == LEFT else (seats, 3 * seats)
+        for i in range(2):
+            rows = slice(starts[i], starts[i] + seats)
+            for j, m in enumerate(own_elems[side]):
+                value = u_high[rows, there(m)].astype(F32) + u_low[rows, there(m)].astype(F32)
+                value = value + spill_in[side][i * seats : (i + 1) * seats, here(j)]
+                put_rows(starts[i], m, value)
 
     def lanes_of(side, halo):
         if halo:
@@ -367,6 +435,8 @@
         answer_out[1] = to_right
         for copy in answer_copies:
             copy.start()
+        for side in (core, away):
+            merge(side)
         for copy in answer_copies:
             copy.wait_recv()
         from_left, beyond_left = answer_in[0], answer_in[1]
@@ -380,16 +450,9 @@
         def returned(lanes):
             return product3(stack, u_high[:, lanes], u_low[:, lanes], False)
 
-        out[away][last] = returned(lanes_of(away, True))
-        out_across(away).start()
-        adjoint[STEPS, :, own[away]] = returned(lanes_of(away, False))
-        backward(away).start()
-        out[core][0] = returned(lanes_of(core, True))
-        out_copy(0, core).start()
-        value = returned(lanes_of(core, False))
-        out_copy(0, 1 - core).wait_recv()
-        adjoint[STEPS, :, own[core]] = value + back[core][0]
-        backward(core).start()
+        for side in (away, core):
+            adjoint[STEPS, :, own[side]] = returned(lanes_of(side, False))
+            backward(side).start()
         readings[column] = jnp.where(near, lower, 0.0)
 
     @pl.when(section == 1)
@@ -399,6 +462,11 @@
 
     @pl.when(section == 0)
     def _():
+        take_weights()
+        weights_high, weights_low = halves(weights_ref[...])
+        station_row = jnp.full((cols, LANES), -1, jnp.int32)
+        for i in range(stats):
+            station_row = jnp.where(lane_ids == i, stations[i], station_row)
         reading = jnp.zeros((cols, LANES), F32)
         for e in range(elems):
             stack = jnp.concatenate(halves(state[STEPS, :, here(e)]), axis=0)
@@ -439,52 +507,32 @@
 
     project()
 
-    def spread(e, low, high):
-        return product3(
-            field[:, here(e)], blocks(jac_high[e], low - e, high - e),
-            blocks(jac_low[e], low - e, high - e), False,
-        )
-
     def send_out(t, side, away):
         put_field(own[side].start, adjoint[t, :, own[side]])
         ref = out[side]
-        if side == LEFT:
-            ref[t] = spread(0, 0, radius)
-            for e in range(1, radius):
-                ref[t, :, e * order :] = ref[t, :, e * order :] + spread(e, e, radius)
-        else:
-            ref[t] = spread(elems - 1, edge, edge + radius)
-            for e in range(elems - radius, elems - 1):
-                size = (e + nbrs - edge) * order
-                ref[t, :, :size] = ref[t, :, :size] + spread(e, edge, e + nbrs)
+        start = -radius if side == LEFT else elems
+        for j in range(radius):
+            value = by_block(field, cols, own_elems[side], start + j)
+            if t == last and away:
+                for part in range(2):
+                    half_lanes = slice(part * half, (part + 1) * half)
+                    out_half[part, :, j * half : (j + 1) * half] = value[:, half_lanes]
+            else:
+                ref[t, :, here(j)] = value
         if t == last and away:
             for part in range(2):
-                for j in range(radius):
-                    lanes = slice(j * order + part * half, j * order + (part + 1) * half)
-                    out_half[part, :, j * half : (j + 1) * half] = ref[t, :, lanes]
                 half_copy(part, side).start()
         else:
             out_copy(t, side).start()
 
-    def begin_adjoint(core, away):
-        for side in (away, core):
-            lanes = own[side]
-            backward(side).wait_recv()
-            total = adjoint_in[:, lanes] + observed[:, lanes]
-            if side == away:
-                out_across(1 - side).wait_recv()
-                total = total + back_across[...]
-            adjoint[0, :, lanes] = total
-            send_out(0, side, side == away)
-
-    def inner(t, side):
-        begin, end = own_span[side]
-        lanes = own[side]
-        adjoint[t + 1, :, lanes] = adjoint[t, :, lanes]
-        for e in range(elems):
-            low, high = max(e, begin), min(e + nbrs, end)
-            lanes = slice((low - radius) * order, (high - radius) * order)
-            adjoint[t + 1, :, lanes] = adjoint[t + 1, :, lanes] + spread(e, low, high)
+    def inner(t, side, first):
+        for m in range(elems):
+            value = by_block(field, cols, own_elems[side], m)
+            if m in own_elems[side]:
+                value = value + adjoint[t, :, here(m)]
+            if not first:
+                value = value + adjoint[t + 1, :, here(m)]
+            adjoint[t + 1, :, here(m)] = value
 
     def add_back(t, side):
         lanes = own[side]
@@ -500,14 +548,19 @@
         return adjoint[STEPS, :, e * order : e * order + half]
 
     def adjoint_step(t, core, away):
-        if t < last:
-            for side in (core, away):
-                add_back(t, side)
-                send_out(t + 1, side, side == away)
-        else:
-            inner(t, away)
+        order_of_sides = (away, core) if t == 0 else (core, away)
+        for side in order_of_sides:
+            if t == 0:
+                lanes = own[side]
+                backward(side).wait_recv()
+                total = adjoint_in[:, lanes] + observed[:, lanes]
+                adjoint[0, :, lanes] = total
+            else:
+                add_back(t - 1, side)
+            send_out(t, side, side == away)
+            inner(t, side, side == order_of_sides[0])
+        if t == last:
             send_up(away)
-            inner(t, core)
             add_back(t, core)
             send_up(core)
             for e in own_elems[core]:
@@ -518,11 +571,7 @@
 
     @pl.when(section == 0)
     def _():
-        by_parity(begin_adjoint)
         for t in range(STEPS):
-            if t < last:
-                inner(t, LEFT)
-                inner(t, RIGHT)
             by_parity(functools.partial(adjoint_step, t))
 
     gram_copy.wait_recv()
@@ -547,12 +596,12 @@
         @pl.when(section == 1)
         def _():
             halo_copy(0, core).wait_send()
-            out_copy(0, core).wait_send()
-            out_across(away).wait_send()
             for copy in answer_copies:
                 copy.wait_send()
             for side in (core, away):
                 once_copy(side).wait_send()
+                for part in (True, False):
+                    spill_copy(side, part).wait_send()
                 backward(side).wait_send()
                 up(side).wait_recv()
             for e in own_elems[core]:
@@ -581,7 +630,7 @@
     slots = max(n_col, LANES // cols)
     sizes = (cols, elems, order, nbrs, stats, n_elem, n_col)
     full, width = elems * order, radius * order
-    copies = 4 * STEPS + 17 + (n_col - 1) + rounds
+    copies = 4 * STEPS + 20 + (n_col - 1) + rounds
     seats = LANES // 2
     scratch = [pltpu.VMEM((nbrs, order, order), F32)] * elems
     scratch += [pltpu.VMEM((order, nbrs * order), BF16)] * (2 * elems)
@@ -599,7 +648,6 @@
         pltpu.VMEM((STEPS, cols, width), F32),
         pltpu.VMEM((STEPS, cols, width), F32),
         pltpu.VMEM((STEPS, cols, width), F32),
-        pltpu.VMEM((cols, width), F32),
         pltpu.VMEM((2, cols, width // 2), F32),
         pltpu.VMEM((cols, width // 2), F32),
         pltpu.VMEM((slots, cols, LANES), F32),
@@ -615,13 +663,18 @@
         pltpu.VMEM((2 * seats, full), BF16),
         pltpu.VMEM((seats, width), F32),
         pltpu.VMEM((seats, width), F32),
+        pltpu.VMEM((2 * seats, width), F32),
+        pltpu.VMEM((2 * seats, width), F32),
+        pltpu.VMEM((2 * seats, width), F32),
+        pltpu.VMEM((2 * seats, width), F32),
         pltpu.VMEM((2, cols, LANES), F32),
         pltpu.VMEM((4, cols, LANES), F32),
-        pltpu.SemaphoreType.DMA((elems + 2,)),
+        pltpu.SMEM((elems, nbrs), jnp.int32),
+        pltpu.SMEM((stats,), jnp.int32),
+        pltpu.SemaphoreType.DMA((elems + 4,)),
         pltpu.SemaphoreType.DMA((copies,)),
         pltpu.SemaphoreType.DMA((copies,)),
     ]
-    smem = pl.BlockSpec(memory_space=pltpu.SMEM)
     anywhere = pl.BlockSpec(memory_space=pl.ANY)
     vmem = pl.BlockSpec(memory_space=pltpu.VMEM)
     hess, gram = pl.pallas_call(
@@ -630,7 +683,7 @@
             jax.ShapeDtypeStruct((elems, cols, order // 2), F32),
             jax.ShapeDtypeStruct((cols, slots * cols), F32),
         ),
-        in_specs=[smem, smem, anywhere, anywhere, anywhere],
+        in_specs=[anywhere] * 5,
         out_specs=(vmem, vmem),
         scratch_shapes=scratch,
         compiler_params=pltpu.CompilerParams(

time: 48.1 us -> 45.2 us (0.940)
  Pallas kernels: 47.2 us -> 44.4 us
    pallas_call x1, Pallas kernels: 45.7 us -> 42.8 us  [per_device(): pl.pallas_call(functools.partial(kernel, sizes), out_shape=(jax.ShapeDtyp...]
where the time goes in v2:
time: 45.2 us; the launch traced here: 45 us
  Pallas kernels  44.4 us (98%)
  between operations  0.64 us (1%)
    pallas_call x1, Pallas kernels, per_device(): pl.pallas_call(functools.partial(kernel, sizes), out_shape=(jax.ShapeDtyp...  42.8 us
    pallas_call x1, Pallas kernels, per_device(): pl.pallas_call(hand_over, out_shape=(jax.ShapeDtypeStruct(hess.shape, F32...  1.55 us

profile of v2, /device:TPU:0, one launch (start us, length us, event | category | flops | bytes accessed | tf_op | source)
XLA Modules:
  0.0 45.0 jit_solution(2759118435378856227)
XLA Ops:
  0.6 42.8 %shard_map.68 = (f32[6,32,128]{2,1,0:T(8,128)}, f32[32,128]{1,0:T(8,128)}) custom-call(s32[6,7]{1,0:T(8,128)} %neighbors_hbm.1, s32[64]{0:T(128)} %stations_hbm.1, f32[6,32,256]{2,1,0:T(8,128)} %bitcast.2, f32[1,6,7,256,256]{4,3,2,1,0:T(8,128)} %jacobian_hbm.1, f32[64,256]{1,0:T(8,128)} %weights_hbm.1), custom_call_target="tpu_custom_call" | custom-call | tf_op jit(solution)/shard_map/pallas_call | solution.py:680
  43.5 1.5 %shard_map.69 = (f32[6,32,128]{2,1,0:T(8,128)}, f32[32,64]{1,0:T(8,128)}) custom-call(f32[6,32,128]{2,1,0:T(8,128)} %get-tuple-element.6.hess_ref, f32[32,128]{1,0:T(8,128)} %get-tuple-element.7.gram_ref), custom_call_target="tpu_custom_call" | custom-call | tf_op jit(solution)/shard_map/pallas_call | solution.py:693

commit v3 on v2

--- a/solution.py
+++ b/solution.py
@@ -58,7 +58,7 @@
         out_half, back_half, readings, partial, partial_in, upper, upper_in,
         u_high, u_low, placed_field, once, once_field, once_halo, once_left, once_right,
         spill_left, spill_right, spill_in_left, spill_in_right,
-        answer_out, answer_in, neighbors, stations,
+        answer_out, answer_in, answer_far, answer_far_in, neighbors, stations,
         load_sem, send_sem, recv_sem,
     ) = scratch[3 * elems :]
     section = lax.axis_index("sec")
@@ -196,9 +196,14 @@
         )
 
     answer_copies = [
-        remote(answer_out.at[part], answer_in.at[slot], ANSWER + slot, {"elem": target})
-        for slot, (part, target) in enumerate(
-            ((1, right), (1, second_right), (0, left), (0, second_left))
+        remote(source.at[part], target.at[slot], ANSWER + index, {"elem": place})
+        for index, (source, target, part, slot, place) in enumerate(
+            (
+                (answer_out, answer_in, 1, 0, right),
+                (answer_out, answer_in, 0, 1, left),
+                (answer_far, answer_far_in, 1, 0, second_right),
+                (answer_far, answer_far_in, 0, 1, second_left),
+            )
         )
     ]
 
@@ -226,16 +231,15 @@
     for load in table_loads:
         load.wait()
 
-    def split(e, use):
-        for d in range(nbrs):
-            target = lax.rem(first_elem + e + d - radius + elem_total, elem_total)
-            slot = jnp.int32(0)
-            for k in range(1, nbrs):
-                slot = jnp.where(neighbors[e, k] == target, jnp.int32(k), slot)
-            high, low = halves(jac_f32[e][slot])
-            jac_high[e][:, d * order : (d + 1) * order] = high
-            jac_low[e][:, d * order : (d + 1) * order] = low
-            use(e + d - radius, high, low)
+    def split(e, d, use):
+        target = lax.rem(first_elem + e + d - radius + elem_total, elem_total)
+        slot = jnp.int32(0)
+        for k in range(1, nbrs):
+            slot = jnp.where(neighbors[e, k] == target, jnp.int32(k), slot)
+        high, low = halves(jac_f32[e][slot])
+        jac_high[e][:, d * order : (d + 1) * order] = high
+        jac_low[e][:, d * order : (d + 1) * order] = low
+        use(e + d - radius, high, low)
 
     lane_ids = lax.broadcasted_iota(jnp.int32, (cols, LANES), 1)
 
@@ -261,14 +265,20 @@
     def here(e):
         return slice(e * order, (e + 1) * order)
 
-    def advance(t, e):
-        added = gathered(e, max(e, radius), min(e + nbrs, edge))
-        state[t + 1, :, here(e)] = state[t, :, here(e)] + added
+    def advance(t, side):
+        ends = [(e, max(e, radius), min(e + nbrs, edge)) for e in own_elems[side]]
+        ends.sort(key=lambda span: span[2] - span[1])
+        e, low, high = ends.pop()
+        middle = (low + high) // 2
+        spans = [ends[1], ends[0], (e, low, middle), (e, middle, high)]
+        for i, (e, low, high) in enumerate(spans):
+            before = state[t + 1 if i == 3 else t, :, here(e)]
+            state[t + 1, :, here(e)] = before + gathered(e, low, high)
 
     def finish_tangent(t, side, away):
         halo_copy(t, 1 - side).wait_recv()
         put_field(0 if side == LEFT else width + full, halo_in[side][t])
-        for e in own_elems[side]:
+        for e in (own_elems[side][1], own_elems[side][0], own_elems[side][2]):
             span = (e, radius) if side == LEFT else (edge, e + nbrs)
             state[t + 1, :, here(e)] = state[t + 1, :, here(e)] + gathered(e, *span)
         if t < last:
@@ -283,27 +293,30 @@
             put_field(width, state[t])
         for side in (away, core) if t == 0 else (core, away):
             if t > 0:
-                for e in own_elems[side]:
-                    advance(t, e)
+                advance(t, side)
             finish_tangent(t, side, side == away)
 
     @pl.when(section == 0)
     def _():
         put_field(width, state[0])
-        for e in range(elems):
-            jac_loads[e].wait()
-            terms = [None, None]
-
-            def use(m, high, low):
+        for pair in range(0, elems, 2):
+            terms = {}
+            for e in range(pair, pair + 2):
+                jac_loads[e].wait()
+
+            def use(e, m, high, low):
                 if 0 <= m < elems:
                     source = blocks(field, m + radius, m + radius + 1)
-                    pair = product(source, high, True), product(source[:cols], low, True)
+                    both = product(source, high, True), product(source[:cols], low, True)
                     for i in range(2):
-                        terms[i] = pair[i] if terms[i] is None else terms[i] + pair[i]
-
-            split(e, use)
-            added = terms[0][:cols] + (terms[0][cols:] + terms[1])
-            state[1, :, here(e)] = state[0, :, here(e)] + added
+                        terms[e, i] = terms[e, i] + both[i] if (e, i) in terms else both[i]
+
+            for d in range(nbrs):
+                for e in range(pair, pair + 2):
+                    split(e, d, functools.partial(use, e))
+            for e in range(pair, pair + 2):
+                added = terms[e, 0][:cols] + (terms[e, 0][cols:] + terms[e, 1])
+                state[1, :, here(e)] = state[0, :, here(e)] + added
         for t in range(STEPS):
             by_parity(functools.partial(tangent, t))
 
@@ -358,7 +371,8 @@
                     value = value + once[:, there(m)]
                 once[:, there(m)] = value
 
-            split(e, use)
+            for d in range(nbrs):
+                split(e, d, use)
             if e == radius - 1:
                 once_copy(LEFT).start()
         once_copy(RIGHT).start()
@@ -413,8 +427,52 @@
             start = width + own[side].start
         return slice(start, start + width)
 
-    def answered(lanes):
-        return product3(field[:, lanes], u_high[:, lanes], u_low[:, lanes], True)
+    def answered(value, lanes):
+        stack = jnp.concatenate(halves(value), axis=0)
+        return product3(stack, u_high[:, lanes], u_low[:, lanes], True)
+
+    def packed(value, keep):
+        rows = cols // 2
+        return jnp.where(keep, value[:rows], pltpu.roll(value[rows:], seats, 1))
+
+    def unpacked(value):
+        return jnp.concatenate([value, pltpu.roll(value, seats, 1)], axis=0)
+
+    for slot in range(n_col, readings.shape[0]):
+        readings[slot] = jnp.zeros((cols, LANES), F32)
+    read_copies = [
+        remote(
+            readings.at[column], readings.at[column], READ + j - 1,
+            {"col": lax.rem(column + j, n_col)},
+        )
+        for j in range(1, n_col)
+    ]
+    flip_copies = [
+        remote(partial.at[r], partial_in.at[r], FLIP + r, flips[r]) for r in range(rounds)
+    ]
+    gram_copy = remote(partial.at[rounds], partial_in.at[rounds], GRAM, {"sec": other})
+
+    def share(reading):
+        readings[column] = reading
+        for copy in read_copies:
+            copy.start()
+
+    def begin_projection():
+        for copy in read_copies:
+            copy.wait_recv()
+        everyone = readings[...].reshape(readings.shape[0] * cols, LANES)
+        high, low = halves(everyone)
+        stack = jnp.concatenate(halves(readings[column]), axis=0)
+        partial[0] = product3(stack, high, low, True)
+        flip_copies[0].start()
+
+    def end_projection():
+        for r in range(rounds):
+            flip_copies[r].wait_recv()
+            partial[r + 1] = partial[r] + partial_in[r]
+            if r + 1 < rounds:
+                flip_copies[r + 1].start()
+        gram_copy.start()
 
     def respond(core, away):
         total = None
@@ -422,38 +480,41 @@
             forward(side).wait_recv()
             if side == core:
                 halo_copy(0, core).start()
-            put_field(width + own[side].start, state[0, :, own[side]])
-            part = answered(lanes_of(side, False))
+            part = answered(state[0, :, own[side]], lanes_of(side, False))
             total = part if total is None else total + part
             halo_copy(0, 1 - side).wait_recv()
-            put_field(lanes_of(side, True).start, halo_in[side][0])
-            total = total + answered(lanes_of(side, True))
+            total = total + answered(halo_in[side][0], lanes_of(side, True))
         near = lane_ids < seats
         to_left = total[:, :LANES]
         to_right = total[:, LANES:] + jnp.where(near, pltpu.roll(to_left, seats, 1), 0.0)
         answer_out[0] = to_left
         answer_out[1] = to_right
+        near_half = near[: cols // 2]
+        answer_far[0] = packed(to_left, near_half)
+        answer_far[1] = packed(to_right, jnp.logical_not(near_half))
         for copy in answer_copies:
             copy.start()
         for side in (core, away):
             merge(side)
         for copy in answer_copies:
             copy.wait_recv()
-        from_left, beyond_left = answer_in[0], answer_in[1]
-        from_right, beyond_right = answer_in[2], answer_in[3]
+        from_left, from_right = answer_in[0], answer_in[1]
+        beyond_left, beyond_right = unpacked(answer_far_in[0]), unpacked(answer_far_in[1])
         upper_half = from_left + to_left
         upper_half = upper_half + pltpu.roll(jnp.where(near, from_right, beyond_left), seats, 1)
         lower = from_right + to_right
         lower = lower + pltpu.roll(jnp.where(near, beyond_right, from_left), seats, 1)
+        share(jnp.where(near, lower, 0.0))
         stack = jnp.concatenate(halves(jnp.concatenate([upper_half, lower], axis=1)), axis=0)
-
-        def returned(lanes):
-            return product3(stack, u_high[:, lanes], u_low[:, lanes], False)
-
         for side in (away, core):
-            adjoint[STEPS, :, own[side]] = returned(lanes_of(side, False))
+            lanes = lanes_of(side, False)
+            answer = product3(stack, u_high[:, lanes], u_low[:, lanes], False)
+            adjoint[STEPS, :, own[side]] = answer
+            if side == core:
+                begin_projection()
+                backward(away).wait_send()
             backward(side).start()
-        readings[column] = jnp.where(near, lower, 0.0)
+        end_projection()
 
     @pl.when(section == 1)
     def _():
@@ -475,37 +536,9 @@
             reading = reading + read
             stack = jnp.concatenate(halves(read), axis=0)
             observed[:, here(e)] = product3(stack, weights_high, weights_low, False)
-        readings[column] = reading
-
-    for slot in range(n_col, readings.shape[0]):
-        readings[slot] = jnp.zeros((cols, LANES), F32)
-    read_copies = [
-        remote(
-            readings.at[column], readings.at[column], READ + j - 1,
-            {"col": lax.rem(column + j, n_col)},
-        )
-        for j in range(1, n_col)
-    ]
-    for copy in read_copies:
-        copy.start()
-    gram_copy = remote(partial.at[rounds], partial_in.at[rounds], GRAM, {"sec": other})
-
-    def project():
-        for copy in read_copies:
-            copy.wait_recv()
-        everyone = readings[...].reshape(readings.shape[0] * cols, LANES)
-        high, low = halves(everyone)
-        stack = jnp.concatenate(halves(readings[column]), axis=0)
-        partial[0] = product3(stack, high, low, True)
-        for r in range(rounds):
-            copy = remote(partial.at[r], partial_in.at[r], FLIP + r, flips[r])
-            copy.start()
-            copy.wait_recv()
-            partial[r + 1] = partial[r] + partial_in[r]
-            copy.wait_send()
-        gram_copy.start()
-
-    project()
+        share(reading)
+        begin_projection()
+        end_projection()
 
     def send_out(t, side, away):
         put_field(own[side].start, adjoint[t, :, own[side]])
@@ -602,7 +635,8 @@
                 once_copy(side).wait_send()
                 for part in (True, False):
                     spill_copy(side, part).wait_send()
-                backward(side).wait_send()
+                if side == core:
+                    backward(side).wait_send()
                 up(side).wait_recv()
             for e in own_elems[core]:
                 hess_ref[e] = upper_in[e]
@@ -612,7 +646,7 @@
 
     by_parity(close)
     gram_copy.wait_send()
-    for copy in read_copies:
+    for copy in read_copies + flip_copies:
         copy.wait_send()
 
 
@@ -668,7 +702,9 @@
         pltpu.VMEM((2 * seats, width), F32),
         pltpu.VMEM((2 * seats, width), F32),
         pltpu.VMEM((2, cols, LANES), F32),
-        pltpu.VMEM((4, cols, LANES), F32),
+        pltpu.VMEM((2, cols, LANES), F32),
+        pltpu.VMEM((2, cols // 2, LANES), F32),
+        pltpu.VMEM((2, cols // 2, LANES), F32),
         pltpu.SMEM((elems, nbrs), jnp.int32),
         pltpu.SMEM((stats,), jnp.int32),
         pltpu.SemaphoreType.DMA((elems + 4,)),

time: 45.2 us -> 44.1 us (0.976)
  Pallas kernels: 44.4 us -> 43.3 us
    pallas_call x1, Pallas kernels: 42.8 us -> 41.8 us  [per_device(): pl.pallas_call(functools.partial(kernel, sizes), out_shape=(jax.ShapeDtyp...]
where the time goes in v3:
time: 44.1 us; the launch traced here: 43.9 us
  Pallas kernels  43.3 us (98%)
  between operations  0.64 us (1%)
    pallas_call x1, Pallas kernels, per_device(): pl.pallas_call(functools.partial(kernel, sizes), out_shape=(jax.ShapeDtyp...  41.8 us
    pallas_call x1, Pallas kernels, per_device(): pl.pallas_call(hand_over, out_shape=(jax.ShapeDtypeStruct(hess.shape, F32...  1.55 us

profile of v3, /device:TPU:0, one launch (start us, length us, event | category | flops | bytes accessed | tf_op | source)
XLA Modules:
  0.0 43.9 jit_solution(8562575409468902881)
XLA Ops:
  0.6 41.8 %shard_map.68 = (f32[6,32,128]{2,1,0:T(8,128)}, f32[32,128]{1,0:T(8,128)}) custom-call(s32[6,7]{1,0:T(8,128)} %neighbors_hbm.1, s32[64]{0:T(128)} %stations_hbm.1, f32[6,32,256]{2,1,0:T(8,128)} %bitcast.2, f32[1,6,7,256,256]{4,3,2,1,0:T(8,128)} %jacobian_hbm.1, f32[64,256]{1,0:T(8,128)} %weights_hbm.1), custom_call_target="tpu_custom_call" | custom-call | tf_op jit(solution)/shard_map/pallas_call | solution.py:716
  42.4 1.5 %shard_map.69 = (f32[6,32,128]{2,1,0:T(8,128)}, f32[32,64]{1,0:T(8,128)}) custom-call(f32[6,32,128]{2,1,0:T(8,128)} %get-tuple-element.6.hess_ref, f32[32,128]{1,0:T(8,128)} %get-tuple-element.7.gram_ref), custom_call_target="tpu_custom_call" | custom-call | tf_op jit(solution)/shard_map/pallas_call | solution.py:729

commit v4 on v3

--- a/solution.py
+++ b/solution.py
@@ -59,6 +59,7 @@
         u_high, u_low, placed_field, once, once_field, once_halo, once_left, once_right,
         spill_left, spill_right, spill_in_left, spill_in_right,
         answer_out, answer_in, answer_far, answer_far_in, neighbors, stations,
+        lower_part,
         load_sem, send_sem, recv_sem,
     ) = scratch[3 * elems :]
     section = lax.axis_index("sec")
@@ -155,6 +156,7 @@
     ONCE = FLIP + rounds
     ANSWER = ONCE + 2
     SPILL = ANSWER + 4
+    PART = SPILL + 4
 
     def halo_copy(t, side):
         return remote(
@@ -206,6 +208,12 @@
             )
         )
     ]
+
+    def backward_part(side, j):
+        lanes = pl.ds(own[side].start + j * order, order)
+        return remote(
+            adjoint.at[STEPS, :, lanes], adjoint_in.at[:, lanes], PART + j, {"sec": other}
+        )
 
     def backward(side):
         return remote(
@@ -291,7 +299,7 @@
     def tangent(t, core, away):
         if t > 0:
             put_field(width, state[t])
-        for side in (away, core) if t == 0 else (core, away):
+        for side in (LEFT, RIGHT) if t == 0 else (core, away):
             if t > 0:
                 advance(t, side)
             finish_tangent(t, side, side == away)
@@ -320,14 +328,16 @@
         for t in range(STEPS):
             by_parity(functools.partial(tangent, t))
 
-    def by_block(source, rows, elements, m):
+    def by_block(source, rows, elements, m, part=None):
         first, second = None, None
         for e in elements:
             if abs(m - e) > radius:
                 continue
-            low = m - e + radius
-            up_term = product(source[:, here(e)], blocks(jac_high[e], low, low + 1), False)
-            low_term = product(source[:rows, here(e)], blocks(jac_low[e], low, low + 1), False)
+            lanes = here(m - e + radius)
+            if part is not None:
+                lanes = slice(lanes.start + part * half, lanes.start + (part + 1) * half)
+            up_term = product(source[:, here(e)], jac_high[e][:, lanes], False)
+            low_term = product(source[:rows, here(e)], jac_low[e][:, lanes], False)
             first = up_term if first is None else first + up_term
             second = low_term if second is None else second + low_term
         return first[:rows] + (first[rows:] + second)
@@ -510,10 +520,13 @@
             lanes = lanes_of(side, False)
             answer = product3(stack, u_high[:, lanes], u_low[:, lanes], False)
             adjoint[STEPS, :, own[side]] = answer
-            if side == core:
+            if side == away:
+                for j in range(radius):
+                    backward_part(away, j).start()
+                backward_part(away, 1).wait_send()
+            else:
+                backward(core).start()
                 begin_projection()
-                backward(away).wait_send()
-            backward(side).start()
         end_projection()
 
     @pl.when(section == 1)
@@ -540,23 +553,12 @@
         begin_projection()
         end_projection()
 
-    def send_out(t, side, away):
+    def send_out(t, side):
         put_field(own[side].start, adjoint[t, :, own[side]])
-        ref = out[side]
         start = -radius if side == LEFT else elems
         for j in range(radius):
-            value = by_block(field, cols, own_elems[side], start + j)
-            if t == last and away:
-                for part in range(2):
-                    half_lanes = slice(part * half, (part + 1) * half)
-                    out_half[part, :, j * half : (j + 1) * half] = value[:, half_lanes]
-            else:
-                ref[t, :, here(j)] = value
-        if t == last and away:
-            for part in range(2):
-                half_copy(part, side).start()
-        else:
-            out_copy(t, side).start()
+            out[side][t, :, here(j)] = by_block(field, cols, own_elems[side], start + j)
+        out_copy(t, side).start()
 
     def inner(t, side, first):
         for m in range(elems):
@@ -572,35 +574,61 @@
         out_copy(t, 1 - side).wait_recv()
         adjoint[t + 1, :, lanes] = adjoint[t + 1, :, lanes] + back[side][t]
 
-    def send_up(side):
-        for e in own_elems[side]:
-            upper[e] = adjoint[STEPS, :, e * order + half : (e + 1) * order]
-        up(side).start()
-
-    def lower_half(e):
-        return adjoint[STEPS, :, e * order : e * order + half]
+    def finish(core, away):
+        add_back(last - 1, away)
+        put_field(own[away].start, adjoint[last, :, own[away]])
+        start = -radius if away == LEFT else elems
+        for j in range(radius):
+            value = by_block(field, cols, own_elems[away], start + j)
+            for part in range(2):
+                half_lanes = slice(part * half, (part + 1) * half)
+                out_half[part, :, j * half : (j + 1) * half] = value[:, half_lanes]
+        for part in range(2):
+            half_copy(part, away).start()
+        for part in (1, 0):
+            for side in (away, core):
+                if side == core and part == 1:
+                    out_copy(last, 1 - core).wait_recv()
+                for j, m in enumerate(own_elems[side]):
+                    lanes = slice(m * order + part * half, m * order + (part + 1) * half)
+                    value = by_block(field, cols, own_elems[away], m, part)
+                    value = value + adjoint[STEPS, :, lanes]
+                    if side == away:
+                        value = value + adjoint[last, :, lanes]
+                    else:
+                        inside = slice(j * order + part * half, j * order + (part + 1) * half)
+                        value = value + back[core][last, :, inside]
+                    if part == 1:
+                        upper[m] = value
+                    elif side == core:
+                        hess_ref[m] = value
+                    else:
+                        lower_part[j] = value
+                if part == 1:
+                    up(side).start()
+        half_copy(0, 1 - away).wait_recv()
+        for j, e in enumerate(own_elems[away]):
+            hess_ref[e] = lower_part[j] + back_half[:, j * half : (j + 1) * half]
 
     def adjoint_step(t, core, away):
         order_of_sides = (away, core) if t == 0 else (core, away)
         for side in order_of_sides:
+            if t == last and side == away:
+                finish(core, away)
+                continue
             if t == 0:
                 lanes = own[side]
-                backward(side).wait_recv()
+                if side == away:
+                    for j in range(radius):
+                        backward_part(away, j).wait_recv()
+                else:
+                    backward(core).wait_recv()
                 total = adjoint_in[:, lanes] + observed[:, lanes]
                 adjoint[0, :, lanes] = total
             else:
                 add_back(t - 1, side)
-            send_out(t, side, side == away)
+            send_out(t, side)
             inner(t, side, side == order_of_sides[0])
-        if t == last:
-            send_up(away)
-            add_back(t, core)
-            send_up(core)
-            for e in own_elems[core]:
-                hess_ref[e] = lower_half(e)
-            half_copy(0, 1 - away).wait_recv()
-            for j, e in enumerate(own_elems[away]):
-                hess_ref[e] = lower_half(e) + back_half[:, j * half : (j + 1) * half]
 
     @pl.when(section == 0)
     def _():
@@ -629,6 +657,9 @@
         @pl.when(section == 1)
         def _():
             halo_copy(0, core).wait_send()
+            for j in range(radius):
+                if j != 1:
+                    backward_part(away, j).wait_send()
             for copy in answer_copies:
                 copy.wait_send()
             for side in (core, away):
@@ -636,7 +667,7 @@
                 for part in (True, False):
                     spill_copy(side, part).wait_send()
                 if side == core:
-                    backward(side).wait_send()
+                    backward(core).wait_send()
                 up(side).wait_recv()
             for e in own_elems[core]:
                 hess_ref[e] = upper_in[e]
@@ -664,7 +695,7 @@
     slots = max(n_col, LANES // cols)
     sizes = (cols, elems, order, nbrs, stats, n_elem, n_col)
     full, width = elems * order, radius * order
-    copies = 4 * STEPS + 20 + (n_col - 1) + rounds
+    copies = 4 * STEPS + 20 + radius + (n_col - 1) + rounds
     seats = LANES // 2
     scratch = [pltpu.VMEM((nbrs, order, order), F32)] * elems
     scratch += [pltpu.VMEM((order, nbrs * order), BF16)] * (2 * elems)
@@ -707,6 +738,7 @@
         pltpu.VMEM((2, cols // 2, LANES), F32),
         pltpu.SMEM((elems, nbrs), jnp.int32),
         pltpu.SMEM((stats,), jnp.int32),
+        pltpu.VMEM((radius, cols, order // 2), F32),
         pltpu.SemaphoreType.DMA((elems + 4,)),
         pltpu.SemaphoreType.DMA((copies,)),
         pltpu.SemaphoreType.DMA((copies,)),

time: 44.1 us -> 43.2 us (0.980)
  Pallas kernels: 43.3 us -> 42.4 us
    pallas_call x1, Pallas kernels: 41.8 us -> 40.9 us  [per_device(): pl.pallas_call(functools.partial(kernel, sizes), out_shape=(jax.ShapeDtyp...]
where the time goes in v4:
time: 43.2 us; the launch traced here: 43 us
  Pallas kernels  42.4 us (98%)
  between operations  0.64 us (1%)
    pallas_call x1, Pallas kernels, per_device(): pl.pallas_call(functools.partial(kernel, sizes), out_shape=(jax.ShapeDtyp...  40.9 us
    pallas_call x1, Pallas kernels, per_device(): pl.pallas_call(hand_over, out_shape=(jax.ShapeDtypeStruct(hess.shape, F32...  1.55 us

profile of v4, /device:TPU:0, one launch (start us, length us, event | category | flops | bytes accessed | tf_op | source)
XLA Modules:
  0.0 43.0 jit_solution(10586011100794794050)
XLA Ops:
  0.6 40.9 %shard_map.68 = (f32[6,32,128]{2,1,0:T(8,128)}, f32[32,128]{1,0:T(8,128)}) custom-call(s32[6,7]{1,0:T(8,128)} %neighbors_hbm.1, s32[64]{0:T(128)} %stations_hbm.1, f32[6,32,256]{2,1,0:T(8,128)} %bitcast.2, f32[1,6,7,256,256]{4,3,2,1,0:T(8,128)} %jacobian_hbm.1, f32[64,256]{1,0:T(8,128)} %weights_hbm.1), custom_call_target="tpu_custom_call" | custom-call | tf_op jit(solution)/shard_map/pallas_call | solution.py:748
  41.5 1.5 %shard_map.69 = (f32[6,32,128]{2,1,0:T(8,128)}, f32[32,64]{1,0:T(8,128)}) custom-call(f32[6,32,128]{2,1,0:T(8,128)} %get-tuple-element.6.hess_ref, f32[32,128]{1,0:T(8,128)} %get-tuple-element.7.gram_ref), custom_call_target="tpu_custom_call" | custom-call | tf_op jit(solution)/shard_map/pallas_call | solution.py:761

commit v5 on v4

--- a/solution.py
+++ b/solution.py
@@ -40,8 +40,9 @@
     probes_hbm,
     jacobian_hbm,
     weights_hbm,
-    hess_ref,
-    gram_ref,
+    hess_hbm,
+    extra_hbm,
+    gram_hbm,
     *scratch,
 ):
     cols, elems, order, nbrs, stats, n_elem, n_col = sizes
@@ -55,11 +56,11 @@
     (
         probes_ref, weights_ref, state, field, halo_left, halo_right,
         adjoint, adjoint_in, observed, out_left, out_right, back_left, back_right,
-        out_half, back_half, readings, partial, partial_in, upper, upper_in,
+        out_half, readings, partial, partial_in, upper,
         u_high, u_low, placed_field, once, once_field, once_halo, once_left, once_right,
         spill_left, spill_right, spill_in_left, spill_in_right,
         answer_out, answer_in, answer_far, answer_far_in, neighbors, stations,
-        lower_part,
+        lower, gram_ref, store_sem,
         load_sem, send_sem, recv_sem,
     ) = scratch[3 * elems :]
     section = lax.axis_index("sec")
@@ -151,12 +152,14 @@
 
     FORWARD = 4 * STEPS
     BACKWARD, UPPER = FORWARD + 2, FORWARD + 4
-    ACROSS, GRAM, LOWER, HIGHER, READ = (FORWARD + 6 + i for i in range(5))
+    GRAM, LOWER, HIGHER, READ = (FORWARD + 6 + i for i in range(4))
     FLIP = READ + n_col - 1
     ONCE = FLIP + rounds
     ANSWER = ONCE + 2
     SPILL = ANSWER + 4
     PART = SPILL + 4
+    ACROSS = PART + radius
+    FORWARD_PART = ACROSS + radius
 
     def halo_copy(t, side):
         return remote(
@@ -164,11 +167,23 @@
             {"elem": neighbour[side]},
         )
 
-    def halo_across(side):
-        return remote(
-            state.at[STEPS, :, own_ds[side]], halo_in[1 - side].at[0], ACROSS,
-            {"sec": other, "elem": neighbour[side]}, side,
-        )
+    def part_lanes(side, j):
+        return pl.ds(own[side].start + j * order, order)
+
+    def across_part(side, j):
+        return remote(
+            state.at[STEPS, :, part_lanes(side, j)], halo_in[1 - side].at[0, :, here_ds(j)],
+            ACROSS + j, {"sec": other, "elem": neighbour[side]},
+        )
+
+    def forward_part(side, j):
+        lanes = part_lanes(side, j)
+        return remote(
+            state.at[STEPS, :, lanes], state.at[0, :, lanes], FORWARD_PART + j, {"sec": other}
+        )
+
+    def here_ds(j):
+        return pl.ds(j * order, order)
 
     def forward(side):
         return remote(
@@ -210,7 +225,7 @@
     ]
 
     def backward_part(side, j):
-        lanes = pl.ds(own[side].start + j * order, order)
+        lanes = part_lanes(side, j)
         return remote(
             adjoint.at[STEPS, :, lanes], adjoint_in.at[:, lanes], PART + j, {"sec": other}
         )
@@ -223,13 +238,13 @@
 
     def half_copy(part, side):
         return remote(
-            out_half.at[part], back_half, (LOWER, HIGHER)[part],
+            out_half.at[part], extra_hbm, (LOWER, HIGHER)[part],
             {"sec": section if part == 0 else other, "elem": neighbour[side]},
         )
 
     def up(side):
         rows = pl.ds(own_elems[side].start, radius)
-        return remote(upper.at[rows], upper_in.at[rows], UPPER + side, {"sec": other})
+        return remote(upper.at[rows], hess_hbm.at[rows], UPPER + side, {"sec": other})
 
     @pl.when(section == 0)
     def _():
@@ -289,12 +304,15 @@
         for e in (own_elems[side][1], own_elems[side][0], own_elems[side][2]):
             span = (e, radius) if side == LEFT else (edge, e + nbrs)
             state[t + 1, :, here(e)] = state[t + 1, :, here(e)] + gathered(e, *span)
+            if t == last and away:
+                j = e - own_elems[side].start
+                forward_part(side, j).start()
+                across_part(side, j).start()
         if t < last:
             halo_copy(t + 1, side).start()
         else:
-            forward(side).start()
-            if away:
-                halo_across(side).start()
+            if not away:
+                forward(side).start()
 
     def tangent(t, core, away):
         if t > 0:
@@ -462,6 +480,18 @@
     ]
     gram_copy = remote(partial.at[rounds], partial_in.at[rounds], GRAM, {"sec": other})
 
+    gram_store = pltpu.make_async_copy(gram_ref, gram_hbm, store_sem.at[2])
+
+    def store(side):
+        rows = pl.ds(own_elems[side].start, radius)
+        return pltpu.make_async_copy(lower.at[rows], hess_hbm.at[rows], store_sem.at[side])
+
+    def store_gram():
+        gram_copy.wait_recv()
+        scale = 1.0 / (elem_total * order)
+        gram_ref[...] = (partial[rounds] + partial_in[rounds]) * scale
+        gram_store.start()
+
     def share(reading):
         readings[column] = reading
         for copy in read_copies:
@@ -484,16 +514,23 @@
                 flip_copies[r + 1].start()
         gram_copy.start()
 
+    def part_slice(side, j):
+        return slice(own[side].start + j * order, own[side].start + (j + 1) * order)
+
     def respond(core, away):
-        total = None
-        for side in (core, away):
-            forward(side).wait_recv()
-            if side == core:
-                halo_copy(0, core).start()
-            part = answered(state[0, :, own[side]], lanes_of(side, False))
-            total = part if total is None else total + part
-            halo_copy(0, 1 - side).wait_recv()
-            total = total + answered(halo_in[side][0], lanes_of(side, True))
+        forward(core).wait_recv()
+        halo_copy(0, core).start()
+        total = answered(state[0, :, own[core]], lanes_of(core, False))
+        halo_copy(0, 1 - core).wait_recv()
+        total = total + answered(halo_in[core][0], lanes_of(core, True))
+        own_start, halo_start = (lanes_of(away, halo).start for halo in (False, True))
+        for j in (1, 0, 2):
+            forward_part(away, j).wait_recv()
+            across_part(1 - away, j).wait_recv()
+            near_lanes = slice(own_start + j * order, own_start + (j + 1) * order)
+            far_lanes = slice(halo_start + j * order, halo_start + (j + 1) * order)
+            total = total + answered(state[0, :, part_slice(away, j)], near_lanes)
+            total = total + answered(halo_in[away][0, :, here(j)], far_lanes)
         near = lane_ids < seats
         to_left = total[:, :LANES]
         to_right = total[:, LANES:] + jnp.where(near, pltpu.roll(to_left, seats, 1), 0.0)
@@ -512,22 +549,23 @@
         beyond_left, beyond_right = unpacked(answer_far_in[0]), unpacked(answer_far_in[1])
         upper_half = from_left + to_left
         upper_half = upper_half + pltpu.roll(jnp.where(near, from_right, beyond_left), seats, 1)
-        lower = from_right + to_right
-        lower = lower + pltpu.roll(jnp.where(near, beyond_right, from_left), seats, 1)
-        share(jnp.where(near, lower, 0.0))
-        stack = jnp.concatenate(halves(jnp.concatenate([upper_half, lower], axis=1)), axis=0)
-        for side in (away, core):
-            lanes = lanes_of(side, False)
+        lower_answer = from_right + to_right
+        lower_answer = lower_answer + pltpu.roll(jnp.where(near, beyond_right, from_left), seats, 1)
+        share(jnp.where(near, lower_answer, 0.0))
+        stack = jnp.concatenate(halves(jnp.concatenate([upper_half, lower_answer], axis=1)), axis=0)
+        for j in range(radius):
+            lanes = slice(own_start + j * order, own_start + (j + 1) * order)
             answer = product3(stack, u_high[:, lanes], u_low[:, lanes], False)
-            adjoint[STEPS, :, own[side]] = answer
-            if side == away:
-                for j in range(radius):
-                    backward_part(away, j).start()
-                backward_part(away, 1).wait_send()
-            else:
-                backward(core).start()
-                begin_projection()
+            adjoint[STEPS, :, part_slice(away, j)] = answer
+            backward_part(away, j).start()
+        lanes = lanes_of(core, False)
+        answer = product3(stack, u_high[:, lanes], u_low[:, lanes], False)
+        adjoint[STEPS, :, own[core]] = answer
+        backward_part(away, 1).wait_send()
+        backward(core).start()
+        begin_projection()
         end_projection()
+        store_gram()
 
     @pl.when(section == 1)
     def _():
@@ -582,7 +620,7 @@
             value = by_block(field, cols, own_elems[away], start + j)
             for part in range(2):
                 half_lanes = slice(part * half, (part + 1) * half)
-                out_half[part, :, j * half : (j + 1) * half] = value[:, half_lanes]
+                out_half[part, j] = value[:, half_lanes]
         for part in range(2):
             half_copy(part, away).start()
         for part in (1, 0):
@@ -600,15 +638,14 @@
                         value = value + back[core][last, :, inside]
                     if part == 1:
                         upper[m] = value
-                    elif side == core:
-                        hess_ref[m] = value
                     else:
-                        lower_part[j] = value
+                        lower[m] = value
                 if part == 1:
                     up(side).start()
+                else:
+                    store(side).start()
+        store_gram()
         half_copy(0, 1 - away).wait_recv()
-        for j, e in enumerate(own_elems[away]):
-            hess_ref[e] = lower_part[j] + back_half[:, j * half : (j + 1) * half]
 
     def adjoint_step(t, core, away):
         order_of_sides = (away, core) if t == 0 else (core, away)
@@ -635,10 +672,6 @@
         for t in range(STEPS):
             by_parity(functools.partial(adjoint_step, t))
 
-    gram_copy.wait_recv()
-    scale = 1.0 / (elem_total * order)
-    gram_ref[...] = (partial[rounds] + partial_in[rounds]) * scale
-
     def close(core, away):
         @pl.when(section == 0)
         def _():
@@ -647,10 +680,13 @@
                     halo_copy(t, side).wait_send()
                     if t < last or side == core:
                         out_copy(t, side).wait_send()
-            halo_across(away).wait_send()
+            forward(core).wait_send()
+            for j in range(radius):
+                across_part(away, j).wait_send()
+                forward_part(away, j).wait_send()
             for side in (core, away):
-                forward(side).wait_send()
                 up(side).wait_send()
+                store(side).wait()
             for part in range(2):
                 half_copy(part, away).wait_send()
 
@@ -669,20 +705,21 @@
                 if side == core:
                     backward(core).wait_send()
                 up(side).wait_recv()
-            for e in own_elems[core]:
-                hess_ref[e] = upper_in[e]
             half_copy(1, 1 - away).wait_recv()
-            for j, e in enumerate(own_elems[away]):
-                hess_ref[e] = upper_in[e] + back_half[:, j * half : (j + 1) * half]
 
     by_parity(close)
     gram_copy.wait_send()
+    gram_store.wait()
     for copy in read_copies + flip_copies:
         copy.wait_send()
 
 
-def hand_over(hess_ref, gram_ref, hess_out, gram_out):
+def hand_over(radius, hess_ref, extra_ref, gram_ref, hess_out, gram_out):
+    elems = hess_ref.shape[0]
+    odd = lax.rem(lax.axis_index("elem"), 2)
     hess_out[...] = hess_ref[...]
+    rows = pl.ds(odd * (elems - radius), radius)
+    hess_out[rows] = hess_ref[rows] + extra_ref[...]
     gram_out[...] = gram_ref[:, : gram_out.shape[1]]
 
 
@@ -695,7 +732,7 @@
     slots = max(n_col, LANES // cols)
     sizes = (cols, elems, order, nbrs, stats, n_elem, n_col)
     full, width = elems * order, radius * order
-    copies = 4 * STEPS + 20 + radius + (n_col - 1) + rounds
+    copies = 4 * STEPS + 19 + 3 * radius + (n_col - 1) + rounds
     seats = LANES // 2
     scratch = [pltpu.VMEM((nbrs, order, order), F32)] * elems
     scratch += [pltpu.VMEM((order, nbrs * order), BF16)] * (2 * elems)
@@ -713,12 +750,10 @@
         pltpu.VMEM((STEPS, cols, width), F32),
         pltpu.VMEM((STEPS, cols, width), F32),
         pltpu.VMEM((STEPS, cols, width), F32),
-        pltpu.VMEM((2, cols, width // 2), F32),
-        pltpu.VMEM((cols, width // 2), F32),
+        pltpu.VMEM((2, radius, cols, order // 2), F32),
         pltpu.VMEM((slots, cols, LANES), F32),
         pltpu.VMEM((rounds + 1, cols, slots * cols), F32),
         pltpu.VMEM((rounds + 1, cols, slots * cols), F32),
-        pltpu.VMEM((elems, cols, order // 2), F32),
         pltpu.VMEM((elems, cols, order // 2), F32),
         pltpu.VMEM((4 * seats, full + 2 * width), BF16),
         pltpu.VMEM((4 * seats, full + 2 * width), BF16),
@@ -738,35 +773,38 @@
         pltpu.VMEM((2, cols // 2, LANES), F32),
         pltpu.SMEM((elems, nbrs), jnp.int32),
         pltpu.SMEM((stats,), jnp.int32),
-        pltpu.VMEM((radius, cols, order // 2), F32),
+        pltpu.VMEM((elems, cols, order // 2), F32),
+        pltpu.VMEM((cols, slots * cols), F32),
+        pltpu.SemaphoreType.DMA((3,)),
         pltpu.SemaphoreType.DMA((elems + 4,)),
         pltpu.SemaphoreType.DMA((copies,)),
         pltpu.SemaphoreType.DMA((copies,)),
     ]
     anywhere = pl.BlockSpec(memory_space=pl.ANY)
     vmem = pl.BlockSpec(memory_space=pltpu.VMEM)
-    hess, gram = pl.pallas_call(
+    hess, extra, gram = pl.pallas_call(
         functools.partial(kernel, sizes),
         out_shape=(
             jax.ShapeDtypeStruct((elems, cols, order // 2), F32),
+            jax.ShapeDtypeStruct((radius, cols, order // 2), F32),
             jax.ShapeDtypeStruct((cols, slots * cols), F32),
         ),
         in_specs=[anywhere] * 5,
-        out_specs=(vmem, vmem),
+        out_specs=(anywhere,) * 3,
         scratch_shapes=scratch,
         compiler_params=pltpu.CompilerParams(
             collective_id=0, has_side_effects=True, vmem_limit_bytes=56 * 1024 * 1024
         ),
     )(neighbors, stations, probes.transpose(1, 0, 2), jacobian, obs_weights)
     hess, gram = pl.pallas_call(
-        hand_over,
+        functools.partial(hand_over, radius),
         out_shape=(
             jax.ShapeDtypeStruct(hess.shape, F32),
             jax.ShapeDtypeStruct((cols, n_col * cols), F32),
         ),
-        in_specs=[vmem, vmem],
+        in_specs=[vmem] * 3,
         out_specs=(vmem, vmem),
-    )(hess, gram)
+    )(hess, extra, gram)
     return hess.transpose(1, 0, 2), gram
 
 

time: 43.2 us -> 42.3 us (0.979)
  Pallas kernels: 42.4 us -> 41.6 us
    pallas_call x1, Pallas kernels: 40.9 us -> 40 us  [per_device(): pl.pallas_call(functools.partial(kernel, sizes), out_shape=(jax.ShapeDtyp...]
where the time goes in v5:
time: 42.3 us; the launch traced here: 42.2 us
  Pallas kernels  41.6 us (98%)
  between operations  0.64 us (2%)
    pallas_call x1, Pallas kernels, per_device(): pl.pallas_call(functools.partial(kernel, sizes), out_shape=(jax.ShapeDtyp...  40 us
    pallas_call x1, Pallas kernels, per_device(): pl.pallas_call(functools.partial(hand_over, radius), out_shape=(jax.Shape...  1.58 us

profile of v5, /device:TPU:0, one launch (start us, length us, event | category | flops | bytes accessed | tf_op | source)
XLA Modules:
  0.0 42.2 jit_solution(7811871770840535796)
XLA Ops:
  0.6 40.0 %shard_map.68 = (f32[6,32,128]{2,1,0:T(8,128)}, f32[3,32,128]{2,1,0:T(8,128)}, f32[32,128]{1,0:T(8,128)}) custom-call(s32[6,7]{1,0:T(8,128)} %neighbors_hbm.1, s32[64]{0:T(128)} %stations_hbm.1, f32[6,32,256]{2,1,0:T(8,128)} %bitcast.2, f32[1,6,7,256,256]{4,3,2,1,0:T(8,128)} %jacobian_hbm.1, f32[64,256]{1,0:T(8,128)} %weights_hbm.1), custom_call_target="tpu_custom_call" | custom-call | tf_op jit(solution)/shard_map/pallas_call | solution.py:785
  40.6 1.6 %shard_map.69 = (f32[6,32,128]{2,1,0:T(8,128)}, f32[32,64]{1,0:T(8,128)}) custom-call(f32[6,32,128]{2,1,0:T(8,128)} %get-tuple-element.7.hess_ref, f32[3,32,128]{2,1,0:T(8,128)} %get-tuple-element.8.extra_ref, f32[32,128]{1,0:T(8,128)} %get-tuple-element.9.gram_ref), custom_call_target="tpu_custom_call" | custom-call | tf_op jit(solution)/shard_map/pallas_call | solution.py:799

commit v6 on v5

--- a/solution.py
+++ b/solution.py
@@ -53,6 +53,8 @@
     jac_f32 = scratch[:elems]
     jac_high = scratch[elems : 2 * elems]
     jac_low = scratch[2 * elems : 3 * elems]
+    turned_high = scratch[3 * elems : 4 * elems]
+    turned_low = scratch[4 * elems : 5 * elems]
     (
         probes_ref, weights_ref, state, field, halo_left, halo_right,
         adjoint, adjoint_in, observed, out_left, out_right, back_left, back_right,
@@ -62,7 +64,7 @@
         answer_out, answer_in, answer_far, answer_far_in, neighbors, stations,
         lower, gram_ref, store_sem,
         load_sem, send_sem, recv_sem,
-    ) = scratch[3 * elems :]
+    ) = scratch[5 * elems :]
     section = lax.axis_index("sec")
     column = lax.axis_index("col")
     block = lax.axis_index("elem")
@@ -117,8 +119,18 @@
         pltpu.make_async_copy(jacobian_hbm.at[0, e], jac_f32[e], load_sem.at[e])
         for e in range(elems)
     ]
-    for load in jac_loads:
-        load.start()
+    backwards = (section == 1) & jnp.logical_not(even)
+
+    @pl.when(backwards)
+    def _():
+        for load in reversed(jac_loads):
+            load.start()
+
+    @pl.when(jnp.logical_not(backwards))
+    def _():
+        for load in jac_loads:
+            load.start()
+
 
     barrier = pltpu.get_barrier_semaphore()
     partners = [{"elem": left}, {"elem": right}, {"sec": other}, {"sec": other, "elem": far}]
@@ -254,12 +266,21 @@
     for load in table_loads:
         load.wait()
 
-    def split(e, d, use):
+    def block_at(e, d):
         target = lax.rem(first_elem + e + d - radius + elem_total, elem_total)
         slot = jnp.int32(0)
         for k in range(1, nbrs):
             slot = jnp.where(neighbors[e, k] == target, jnp.int32(k), slot)
-        high, low = halves(jac_f32[e][slot])
+        return jac_f32[e][slot]
+
+    def turn(e, d, use):
+        high, low = halves(block_at(e, d).T)
+        turned_high[e][here(d), :] = high
+        turned_low[e][here(d), :] = low
+        use(e + d - radius, high, low)
+
+    def split(e, d, use):
+        high, low = halves(block_at(e, d))
         jac_high[e][:, d * order : (d + 1) * order] = high
         jac_low[e][:, d * order : (d + 1) * order] = low
         use(e + d - radius, high, low)
@@ -280,9 +301,9 @@
         return ref[:, begin * order : end * order]
 
     def gathered(e, low, high):
+        rows = slice((low - e) * order, (high - e) * order)
         return product3(
-            blocks(field, low, high), blocks(jac_high[e], low - e, high - e),
-            blocks(jac_low[e], low - e, high - e), True,
+            blocks(field, low, high), turned_high[e][rows, :], turned_low[e][rows, :], False
         )
 
     def here(e):
@@ -333,13 +354,13 @@
             def use(e, m, high, low):
                 if 0 <= m < elems:
                     source = blocks(field, m + radius, m + radius + 1)
-                    both = product(source, high, True), product(source[:cols], low, True)
+                    both = product(source, high, False), product(source[:cols], low, False)
                     for i in range(2):
                         terms[e, i] = terms[e, i] + both[i] if (e, i) in terms else both[i]
 
             for d in range(nbrs):
                 for e in range(pair, pair + 2):
-                    split(e, d, functools.partial(use, e))
+                    turn(e, d, functools.partial(use, e))
             for e in range(pair, pair + 2):
                 added = terms[e, 0][:cols] + (terms[e, 0][cols:] + terms[e, 1])
                 state[1, :, here(e)] = state[0, :, here(e)] + added
@@ -385,25 +406,31 @@
             placed_field[:seats, here(e)] = high
             placed_field[seats:, here(e)] = low
 
-        for e in range(elems):
-            jac_loads[e].wait()
-
-            def use(m, high, low, e=e):
-                source = placed_field[:, here(e)]
-                first = product(source, high, False)
-                value = first[seats:] + product(source[:seats], low, False)
-                value = first[:seats] + value
-                if m == e:
-                    value = value + placed(e)
-                if e > 0 and m < e + radius:
-                    value = value + once[:, there(m)]
-                once[:, there(m)] = value
-
-            for d in range(nbrs):
-                split(e, d, use)
-            if e == radius - 1:
-                once_copy(LEFT).start()
-        once_copy(RIGHT).start()
+        def collect(core, away):
+            seen = set()
+            sequence = range(elems) if away == LEFT else range(elems - 1, -1, -1)
+            for i, e in enumerate(sequence):
+                jac_loads[e].wait()
+
+                def use(m, high, low, e=e):
+                    source = placed_field[:, here(e)]
+                    first = product(source, high, False)
+                    value = first[seats:] + product(source[:seats], low, False)
+                    value = first[:seats] + value
+                    if m == e:
+                        value = value + placed(e)
+                    if m in seen:
+                        value = value + once[:, there(m)]
+                    seen.add(m)
+                    once[:, there(m)] = value
+
+                for d in range(nbrs):
+                    split(e, d, use)
+                if i == radius - 1:
+                    once_copy(away).start()
+            once_copy(core).start()
+
+        by_parity(collect)
         for m in range(elems):
             high, low = halves(once[:, there(m)])
             once_field[:seats, here(m)] = high
@@ -588,7 +615,11 @@
             stack = jnp.concatenate(halves(read), axis=0)
             observed[:, here(e)] = product3(stack, weights_high, weights_low, False)
         share(reading)
-        begin_projection()
+        for e in range(elems):
+            for d in range(nbrs):
+                split(e, d, lambda m, high, low: None)
+            if e == radius:
+                begin_projection()
         end_projection()
 
     def send_out(t, side):
@@ -736,6 +767,7 @@
     seats = LANES // 2
     scratch = [pltpu.VMEM((nbrs, order, order), F32)] * elems
     scratch += [pltpu.VMEM((order, nbrs * order), BF16)] * (2 * elems)
+    scratch += [pltpu.VMEM((nbrs * order, order), BF16)] * (2 * elems)
     scratch += [
         pltpu.VMEM((elems, cols, order), F32),
         pltpu.VMEM((LANES, order), F32),

time: 42.3 us -> 40.7 us (0.962)
  Pallas kernels: 41.6 us -> 39.9 us
    pallas_call x1, Pallas kernels: 40 us -> 38.3 us  [per_device(): pl.pallas_call(functools.partial(kernel, sizes), out_shape=(jax.ShapeDtyp...]
where the time goes in v6:
time: 40.7 us; the launch traced here: 40.5 us
  Pallas kernels  39.9 us (98%)
  between operations  0.64 us (2%)
    pallas_call x1, Pallas kernels, per_device(): pl.pallas_call(functools.partial(kernel, sizes), out_shape=(jax.ShapeDtyp...  38.3 us
    pallas_call x1, Pallas kernels, per_device(): pl.pallas_call(functools.partial(hand_over, radius), out_shape=(jax.Shape...  1.58 us

profile of v6, /device:TPU:0, one launch (start us, length us, event | category | flops | bytes accessed | tf_op | source)
XLA Modules:
  0.0 40.5 jit_solution(10847008820297883470)
XLA Ops:
  0.6 38.3 %shard_map.68 = (f32[6,32,128]{2,1,0:T(8,128)}, f32[3,32,128]{2,1,0:T(8,128)}, f32[32,128]{1,0:T(8,128)}) custom-call(s32[6,7]{1,0:T(8,128)} %neighbors_hbm.1, s32[64]{0:T(128)} %stations_hbm.1, f32[6,32,256]{2,1,0:T(8,128)} %bitcast.2, f32[1,6,7,256,256]{4,3,2,1,0:T(8,128)} %jacobian_hbm.1, f32[64,256]{1,0:T(8,128)} %weights_hbm.1), custom_call_target="tpu_custom_call" | custom-call | tf_op jit(solution)/shard_map/pallas_call | solution.py:817
  38.9 1.6 %shard_map.69 = (f32[6,32,128]{2,1,0:T(8,128)}, f32[32,64]{1,0:T(8,128)}) custom-call(f32[6,32,128]{2,1,0:T(8,128)} %get-tuple-element.7.hess_ref, f32[3,32,128]{2,1,0:T(8,128)} %get-tuple-element.8.extra_ref, f32[32,128]{1,0:T(8,128)} %get-tuple-element.9.gram_ref), custom_call_target="tpu_custom_call" | custom-call | tf_op jit(solution)/shard_map/pallas_call | solution.py:831

commit v7 on v6

--- a/solution.py
+++ b/solution.py
@@ -153,7 +153,13 @@
         for e in range(elems):
             state[0, :, e * order : (e + 1) * order] = probes_ref[e]
 
-    pl.semaphore_wait(barrier, len(partners) + len(flips))
+    def everyone_in():
+        pl.semaphore_wait(barrier, len(partners) + len(flips))
+
+    @pl.when(section == 0)
+    def _():
+        everyone_in()
+
 
     def remote(src, dst, index, target, arrival=None):
         arrival = index if arrival is None else arrival
@@ -427,6 +433,7 @@
                 for d in range(nbrs):
                     split(e, d, use)
                 if i == radius - 1:
+                    everyone_in()
                     once_copy(away).start()
             once_copy(core).start()
 

time: 40.7 us -> 40.7 us (level)
  no operation moved by 1% of the time
where the time goes in v7:
time: 40.7 us; the launch traced here: 40.5 us
  Pallas kernels  39.9 us (98%)
  between operations  0.64 us (2%)
    pallas_call x1, Pallas kernels, per_device(): pl.pallas_call(functools.partial(kernel, sizes), out_shape=(jax.ShapeDtyp...  38.3 us
    pallas_call x1, Pallas kernels, per_device(): pl.pallas_call(functools.partial(hand_over, radius), out_shape=(jax.Shape...  1.58 us

profile of v7, /device:TPU:0, one launch (start us, length us, event | category | flops | bytes accessed | tf_op | source)
XLA Modules:
  0.0 40.5 jit_solution(8279467917160624422)
XLA Ops:
  0.6 38.3 %shard_map.68 = (f32[6,32,128]{2,1,0:T(8,128)}, f32[3,32,128]{2,1,0:T(8,128)}, f32[32,128]{1,0:T(8,128)}) custom-call(s32[6,7]{1,0:T(8,128)} %neighbors_hbm.1, s32[64]{0:T(128)} %stations_hbm.1, f32[6,32,256]{2,1,0:T(8,128)} %bitcast.2, f32[1,6,7,256,256]{4,3,2,1,0:T(8,128)} %jacobian_hbm.1, f32[64,256]{1,0:T(8,128)} %weights_hbm.1), custom_call_target="tpu_custom_call" | custom-call | tf_op jit(solution)/shard_map/pallas_call | solution.py:824
  38.9 1.6 %shard_map.69 = (f32[6,32,128]{2,1,0:T(8,128)}, f32[32,64]{1,0:T(8,128)}) custom-call(f32[6,32,128]{2,1,0:T(8,128)} %get-tuple-element.7.hess_ref, f32[3,32,128]{2,1,0:T(8,128)} %get-tuple-element.8.extra_ref, f32[32,128]{1,0:T(8,128)} %get-tuple-element.9.gram_ref), custom_call_target="tpu_custom_call" | custom-call | tf_op jit(solution)/shard_map/pallas_call | solution.py:838
